TPU v7x, 512 devices: a whole 4x4x16 slice. The times are simulated.
512 devices in a mesh: row: 8 (over y, core), col: 8 (over z_lo), depth: 8 (over z_hi, x).
Axes of the slice: x: 4, y: 4, z: 16 (z_hi: 2, z_lo: 8; z = z_hi * 8 + z_lo), core: 2. Of those that a mesh axis runs over, the one named last changes fastest.
Arguments:
- tokens: bfloat16 [1024, 4096], P(('col', 'depth'), 'row'), may hold values from -6 to 6
- out_grad: bfloat16 [1024, 4096], P(('col', 'depth'), 'row'), may hold values from -2 to 2
- w_in: bfloat16 [4096, 14336], P('row', 'col'), may hold values from -0.09375 to 0.09375
- b_in: float32 [14336], P('col'), may hold values from -3 to 3
- w_out: bfloat16 [14336, 4096], P('col', 'row'), may hold values from -0.046875 to 0.046875
Outputs:
- block_out: bfloat16 [1024, 4096], P(('col', 'depth'), 'row')
- tokens_grad: bfloat16 [1024, 4096], P(('col', 'depth'), 'row')
- w_in_grad: bfloat16 [4096, 14336], P('row', ('col', 'depth'))
- w_out_grad: bfloat16 [14336, 4096], P(('col', 'depth'), 'row')
- b_in_grad: float32 [14336], P('col')
All inputs are finite; a program needn't handle non-finite values.
Results may differ from a plain program's by a relative error of at most 0.005.
Values may be sent and summed in bfloat16 or wider, within the bound.
No kernel may reach another device: no remote copies, remote signals or barrier semaphores. Data moves between devices by JAX's collectives and lax.ppermute only.
A program may use at most 64 MiB of HBM per device.

v0:
```python
import jax
import jax.numpy as jnp
from jax import lax
from jax.experimental import pallas as pl
from jax.experimental.pallas import tpu as pltpu
from jax.sharding import Mesh, PartitionSpec as P


root_coeff = 0.7978845608028654
cubic_coeff = 0.044715
f32 = jnp.float32
bf16 = jnp.bfloat16
fine_names = ("y", "core", "zq", "zp", "zh", "x")
fine_shape = (4, 2, 4, 2, 2, 4)


def gelu_parts(pre_act):
    inner_arg = root_coeff * (pre_act + cubic_coeff * pre_act * pre_act * pre_act)
    tangent = jnp.tanh(inner_arg)
    gelu_value = 0.5 * pre_act * (1.0 + tangent)
    gelu_slope = 0.5 * (1.0 + tangent) + 0.5 * pre_act * (1.0 - tangent * tangent) * root_coeff * (
        1.0 + 3.0 * cubic_coeff * pre_act * pre_act
    )
    return (gelu_value, gelu_slope)


def dot_nt(a, b):
    return lax.dot_general(a, b, (((1,), (1,)), ((), ())), preferred_element_type=f32)


def dot_nn(a, b):
    return jnp.dot(a, b, preferred_element_type=f32)


def hi_lo(v):
    hi = v.astype(bf16)
    return hi, (v - hi.astype(f32)).astype(bf16)


def weight_body(place_ref, x0_ref, x1_ref, x2_ref, x3_ref, hid_ref, win_ref, wout_ref, b_ref, h_ref):
    col_n, tall, wide = hid_ref.shape
    part = wide // 2
    half = b_ref.shape[1] // wide
    dep_n = 2 * half
    tile = (tall - dep_n) // dep_n
    x_refs = (x0_ref, x1_ref, x2_ref, x3_ref)
    x_n = len(x_refs)
    zh_n = dep_n // x_n
    my_x = place_ref[1]
    total = jnp.zeros((dep_n, wide), f32)
    for j in range(col_n):
        total = total + hid_ref[j, dep_n * tile :].astype(f32)
    total = total[:half] + total[half:]
    for j in range(half):
        b_ref[:, j * wide : (j + 1) * wide] = total[j : j + 1]
    acc_in = jnp.zeros(win_ref.shape, f32)
    acc_out = jnp.zeros(wout_ref.shape, f32)
    for k, x_ref in enumerate(x_refs):
        src_x = lax.rem(my_x + (x_n - k), x_n)
        for zh in range(zh_n):
            at = pl.multiple_of((zh * x_n + src_x) * tile, tile)
            for j in range(col_n):
                to = (zh * col_n + j) * tile
                h_ref[k, to : to + tile, :] = hid_ref[j, pl.ds(at, tile), :]
        turned = h_ref[k].T
        blk = x_ref[...].reshape(-1, 2, tile, x_ref.shape[-1])
        rows = blk.shape[0] * tile
        acc_out += dot_nn(turned[:part], blk[:, 1].reshape(rows, -1))
        acc_in += dot_nn(turned[part:], blk[:, 0].reshape(rows, -1))
    win_ref[...] = acc_in.astype(bf16)
    wout_ref[...] = acc_out.astype(bf16)


def weight_stage(place, chunks, hid, dep_n):
    _, _, wide = hid.shape
    d_loc = chunks[0].shape[-1]
    vmem = pl.BlockSpec(memory_space=pltpu.VMEM)
    return pl.pallas_call(
        weight_body,
        in_specs=[pl.BlockSpec(memory_space=pltpu.SMEM)] + [vmem] * 5,
        out_specs=(vmem, vmem, vmem),
        out_shape=(
            jax.ShapeDtypeStruct((wide // 2, d_loc), bf16),
            jax.ShapeDtypeStruct((wide // 2, d_loc), bf16),
            jax.ShapeDtypeStruct((1, wide * dep_n // 2), f32),
        ),
        scratch_shapes=[pltpu.VMEM((len(chunks), chunks[0].shape[0] // 2, wide), bf16)],
        name="weight_stage",
    )(place, *chunks, hid)


def step(tokens, out_grad, w_in, b_in, w_out):
    y_n, x_n = lax.axis_size("y"), lax.axis_size("x")
    zh_n = lax.axis_size("zh")
    dep_n = zh_n * x_n
    half = dep_n // 2
    tile, d_loc = tokens.shape
    f_loc = w_in.shape[1]
    part = f_loc // dep_n
    my_core, my_x = lax.axis_index("core"), lax.axis_index("x")
    swap = [(0, 1), (1, 0)]

    both = jnp.concatenate([tokens, out_grad], axis=0)
    zall = lax.all_gather(both, ("zh", "zq", "zp"), axis=0, tiled=True)
    others = []
    for k in range(1, x_n):
        others.append(lax.ppermute(zall, "x", [(i, (i + k) % x_n) for i in range(x_n)]))
    mine = lax.dynamic_index_in_dim(
        zall.reshape(zh_n, y_n, 2, 2, tile, d_loc), lax.axis_index("zh"), 0, keepdims=False
    )

    def first_products(core):
        blk = lax.dynamic_index_in_dim(mine, core, 1, keepdims=False)
        return jnp.concatenate(
            [
                dot_nn(blk[:, 0].reshape(y_n * tile, d_loc), w_in),
                dot_nt(blk[:, 1].reshape(y_n * tile, d_loc), w_out),
            ],
            axis=1,
        )

    from_core = lax.ppermute(first_products(1 - my_core), "core", swap)
    pre = (first_products(my_core) + from_core).astype(bf16)
    pre = lax.all_to_all(pre.reshape(y_n, tile, 2 * f_loc), "y", 0, 0)
    pre = jnp.sum(pre.astype(f32), axis=0)
    value, slope = gelu_parts(pre[:, :f_loc] + b_in)
    pre_grad = pre[:, f_loc:] * slope
    act, hgrad = value.astype(bf16), pre_grad.astype(bf16)
    hid = jnp.concatenate([act, hgrad], axis=1)
    b_rows = jnp.concatenate(hi_lo(jnp.sum(pre_grad, axis=0).reshape(half, 2 * part)), axis=0)
    send = jnp.concatenate(
        [
            act.reshape(tile, dep_n, part).transpose(1, 0, 2),
            hgrad.reshape(tile, dep_n, part).transpose(1, 0, 2),
        ],
        axis=2,
    )
    send = jnp.concatenate([send, jnp.broadcast_to(b_rows, (dep_n,) + b_rows.shape)], axis=1)
    got = lax.all_to_all(send, ("zh", "x"), 0, 0)
    rows = lax.all_gather(hid, ("y", "core"), axis=0, tiled=True)
    outs = jnp.concatenate(
        [dot_nn(rows[:, :f_loc], w_out).astype(bf16), dot_nt(rows[:, f_loc:], w_in).astype(bf16)],
        axis=1,
    )
    outs = lax.all_to_all(outs.reshape(2 * y_n, tile, 2 * d_loc), ("zq", "zp"), 0, 0)
    total = outs[0].astype(f32)
    for j in range(1, 2 * y_n):
        total = total + outs[j].astype(f32)
    block_out, tokens_grad = total[:, :d_loc].astype(bf16), total[:, d_loc:].astype(bf16)

    b_sum = jnp.sum(got[:, tile : tile + half].astype(f32) + got[:, tile + half :].astype(f32), axis=0)
    b_pair = jnp.concatenate(hi_lo(b_sum), axis=0)
    wsend = jnp.concatenate([got[:, :tile].reshape(dep_n * tile, 2 * part), b_pair], axis=0)
    wall = lax.all_gather(wsend, ("y", "core"), axis=0, tiled=False)
    place = jnp.stack([my_core, my_x])
    w_in_grad, w_out_grad, b_in_grad = weight_stage(place, [zall] + others, wall, dep_n)
    return (block_out, tokens_grad, w_in_grad.T, w_out_grad, b_in_grad.reshape(f_loc))


def solution(mesh):
    fine = Mesh(mesh.devices.reshape(fine_shape), fine_names)
    col = ("zq", "zp")
    row = ("y", "core")
    owner = ("zq", "zp", "zh", "x")
    tok = P(owner, row)
    return jax.shard_map(
        step,
        mesh=fine,
        in_specs=(tok, tok, P(row, col), P(col), P(col, row)),
        out_specs=(tok, tok, P(row, owner), P(owner, row), P(col)),
        check_vma=False,
    )
```

profile of v0, /device:TPU:1, one launch (start us, length us, event | category | flops | bytes accessed | tf_op | source)
XLA Modules:
  0.0 133.3 jit_solution(3781854605802463106)
XLA Ops:
  0.6 0.0 copy-start
  0.7 0.9 pad_maximum_fusion.5
  1.5 31.8 %all_gather.12.x0_ref = bf16[512,512]{1,0:T(8,128)(2,1)S(1)} all-gather(bf16[32,512]{1,0:T(8,128)(2,1)S(1)} %pad_maximum_fusion.5), channel_id=1, replica_groups=mesh['y'=4,'core'=2,'zq'=4,'zp'=2,'zh'=2,'x'=4] {'zh','zq','zp'}, dimensions={0}, use_global_device_ids=true | all-gather | bytes 557056 | tf_op jit(solution)/shard_map/all_gather | solution.py:104
  33.3 0.0 copy-start.3
  33.4 2.3 %fusion.18 = f32[64,1792]{1,0:T(8,128)S(1)} fusion(bf16[64,512]{1,0:T(8,128)(2,1)S(1)} %bitcast.38, bf16[1792,512]{1,0:T(8,128)(2,1)} %param.9), kind=kOutput, calls=%fused_computation.39 | convolution fusion | flops 117440512 | bytes 2359296 | tf_op jit(solution)/shard_map/dot_general | solution.py:28
  35.7 0.0 copy-done
  35.7 0.0 copy-start.1
  35.7 0.4 fusion.17
  36.1 0.1 pad_maximum_fusion
  36.2 10.3 %collective-permute-start = (f32[64,3584]{1,0:T(8,128)S(1)}, f32[64,3584]{1,0:T(8,128)S(1)}, u32[]{:S(2)}, u32[]{:S(2)}) collective-permute-start(f32[64,3584]{1,0:T(8,128)S(1)} %pad_maximum_fusion), channel_id=1, source_target_pairs={{0,64},{64,0},{1,65},{65,1},{2,66},{66,2},{3,67},{67,3},{4,68},{68... | collective-permute-start | bytes 2752520 | tf_op jit(solution)/shard_map/ppermute | solution.py:122
  46.5 0.0 copy-done.1
  46.5 0.7 fusion.16
  47.2 0.4 fusion.15
  47.6 0.0 copy-start.4
  47.6 0.9 collective-permute-done
  48.6 0.8 fusion
  49.4 4.2 %all-to-all-start = ((bf16[4,16,3584]{2,1,0:T(8,128)(2,1)}), bf16[4,16,3584]{2,1,0:T(8,128)(2,1)S(1)}, u32[]{:S(2)}, u32[]{:S(2)}) async-start(bf16[4,16,3584]{2,1,0:T(8,128)(2,1)} %bitcast.7), calls=%async_computation | async-start | bytes 917504 | tf_op jit(solution)/shard_map/all_to_all | solution.py:124
  53.6 3.1 %collective-permute-start.1 = (bf16[512,512]{1,0:T(8,128)(2,1)S(1)}, bf16[512,512]{1,0:T(8,128)(2,1)}, u32[]{:S(2)}, u32[]{:S(2)}) collective-permute-start(bf16[512,512]{1,0:T(8,128)(2,1)S(1)} %all_gather.12.x0_ref), channel_id=1, source_target_pairs={{0,1},{1,2},{2,3},{3,0},{4,5},{5,6},{6,7},{7,4},{8,9},{9,10},{10,1... | collective-permute-start | bytes 1572872 | tf_op jit(solution)/shard_map/ppermute | solution.py:107
  56.7 4.4 %collective-permute-start.2 = (bf16[512,512]{1,0:T(8,128)(2,1)S(1)}, bf16[512,512]{1,0:T(8,128)(2,1)}, u32[]{:S(2)}, u32[]{:S(2)}) collective-permute-start(bf16[512,512]{1,0:T(8,128)(2,1)S(1)} %all_gather.12.x0_ref), channel_id=1, source_target_pairs={{0,2},{1,3},{2,0},{3,1},{4,6},{5,7},{6,4},{7,5},{8,10},{9,11},{10,... | collective-permute-start | bytes 1572872 | tf_op jit(solution)/shard_map/ppermute | solution.py:107
  61.1 0.0 copy-done.3
  61.1 3.1 %collective-permute-start.3 = (bf16[512,512]{1,0:T(8,128)(2,1)S(1)}, bf16[512,512]{1,0:T(8,128)(2,1)}, u32[]{:S(2)}, u32[]{:S(2)}) collective-permute-start(bf16[512,512]{1,0:T(8,128)(2,1)S(1)} %all_gather.12.x0_ref), channel_id=1, source_target_pairs={{0,3},{1,0},{2,1},{3,2},{4,7},{5,4},{6,5},{7,6},{8,11},{9,8},{10,9... | collective-permute-start | bytes 1572872 | tf_op jit(solution)/shard_map/ppermute | solution.py:107
  64.2 0.0 all-to-all-done
  64.2 0.1 convert_reduce_fusion
  64.2 0.0 copy-done.4
  64.3 0.1 fusion.10
  64.4 0.1 reshape.58
  64.5 0.1 reshape.57
  64.7 15.7 %all_gather.13 = bf16[128,3584]{1,0:T(8,128)(2,1)S(1)} all-gather(bf16[16,3584]{1,0:T(8,128)(2,1)S(1)} %pad_maximum_fusion.4), channel_id=1, replica_groups=mesh['y'=4,'core'=2,'zq'=4,'zp'=2,'zh'=2,'x'=4] {'y','core'}, dimensions={0}, use_global_device_ids=true | all-gather | bytes 1032192 | tf_op jit(solution)/shard_map/all_gather | solution.py:140
  80.4 0.1 reshape.59
  80.5 0.1 pad_maximum_fusion.2
  80.6 0.7 copy.11
  81.3 6.0 %all-to-all-start.2 = ((bf16[8,24,448]{2,1,0:T(8,128)(2,1)}), bf16[8,24,448]{2,1,0:T(8,128)(2,1)S(1)}, u32[]{:S(2)}, u32[]{:S(2)}) async-start(bf16[8,24,448]{2,1,0:T(8,128)(2,1)} %copy.11), calls=%async_computation.2 | async-start | bytes 393216 | tf_op jit(solution)/shard_map/all_to_all | solution.py:139
  87.4 0.0 copy-start.2
  87.4 0.7 convolution_convert_fusion
  88.1 0.8 copy-done.2
  88.9 0.4 convolution_convert_fusion.1
  89.3 0.7 pad_maximum_fusion.1
  90.0 12.2 %all-to-all-done.2 = bf16[8,24,448]{2,1,0:T(8,128)(2,1)S(1)} async-done(((bf16[8,24,448]{2,1,0:T(8,128)(2,1)}), bf16[8,24,448]{2,1,0:T(8,128)(2,1)S(1)}, u32[]{:S(2)}, u32[]{:S(2)}) %all-to-all-start.2) | async-done | bytes 172064 | tf_op jit(solution)/shard_map/all_to_all | solution.py:139
  102.2 9.3 %all-to-all-start.1 = ((bf16[8,16,1024]{2,1,0:T(8,128)(2,1)}), bf16[8,16,1024]{2,1,0:T(8,128)(2,1)S(1)}, u32[]{:S(2)}, u32[]{:S(2)}) async-start(bf16[8,16,1024]{2,1,0:T(8,128)(2,1)} %bitcast.8), calls=%async_computation.1 | async-start | bytes 524288 | tf_op jit(solution)/shard_map/all_to_all | solution.py:145
  111.5 0.6 pad_add_fusion.place_ref
  112.2 15.8 %all-gather = bf16[1088,448]{1,0:T(8,128)(2,1)} all-gather(bf16[136,448]{1,0:T(8,128)(2,1)S(1)} %pad_maximum_fusion.3), channel_id=2, replica_groups=mesh['y'=4,'core'=2,'zq'=4,'zp'=2,'zh'=2,'x'=4] {'y','core'}, dimensions={0}, use_global_device_ids=true | all-gather | bytes 1096704 | tf_op jit(solution)/shard_map/all_gather | solution.py:154
  128.0 0.0 collective-permute-done.1.x1_ref
  128.0 0.0 collective-permute-done.2.x2_ref
  128.0 0.0 collective-permute-done.3.x3_ref
  128.0 3.3 %weight_stage.1 = (bf16[224,512]{1,0:T(8,128)(2,1)}, bf16[224,512]{1,0:T(8,128)(2,1)}, f32[1,1792]{1,0:T(1,128)}) custom-call(s32[2]{0:T(128)} %pad_add_fusion.place_ref, bf16[512,512]{1,0:T(8,128)(2,1)} %copy-done.3, bf16[512,512]{1,0:T(8,128)(2,1)} %collective-permute-done.1.x1_ref, bf16[512,512]{1,0:T(8,128)(2,1)} %collective-permute-done.2.x2_ref, ...), custom_call_target="tpu_custom_call" | custom-call | tf_op jit(solution)/shard_map/weight_stage/pallas_call | solution.py:78
  131.4 1.3 reduce
  132.7 0.0 all-to-all-done.1
  132.7 0.6 fusion.14
  (11 shorter events, 0.2 us)
Async XLA Ops:
  0.6 35.0 %copy-start = (bf16[512,1792]{1,0:T(8,128)(2,1)S(1)}, bf16[512,1792]{1,0:T(8,128)(2,1)}, u32[]{:S(2)}) copy-start(bf16[512,1792]{1,0:T(8,128)(2,1)} %param.7) | copy-start | bytes 5505028
  33.3 27.8 %copy-start.3 = (bf16[512,512]{1,0:T(8,128)(2,1)}, bf16[512,512]{1,0:T(8,128)(2,1)S(1)}, u32[]{:S(2)}) copy-start(bf16[512,512]{1,0:T(8,128)(2,1)S(1)} %all_gather.12.x0_ref) | copy-start | bytes 1572868
  35.7 10.8 %copy-start.1 = (bf16[1792,512]{1,0:T(8,128)(2,1)S(1)}, bf16[1792,512]{1,0:T(8,128)(2,1)}, u32[]{:S(2)}) copy-start(bf16[1792,512]{1,0:T(8,128)(2,1)} %param.9) | copy-start | bytes 5505028
  36.2 12.4 %collective-permute-start = (f32[64,3584]{1,0:T(8,128)S(1)}, f32[64,3584]{1,0:T(8,128)S(1)}, u32[]{:S(2)}, u32[]{:S(2)}) collective-permute-start(f32[64,3584]{1,0:T(8,128)S(1)} %pad_maximum_fusion), channel_id=1, source_target_pairs={{0,64},{64,0},{1,65},{65,1},{2,66},{66,2},{3,67},{67,3},{4,68},{68... | collective-permute-start | bytes 2752520 | tf_op jit(solution)/shard_map/ppermute | solution.py:122
  47.6 16.6 %copy-start.4 = (f32[1792]{0:T(1024)S(1)}, f32[1792]{0:T(1024)}, u32[]{:S(2)}) copy-start(f32[1792]{0:T(1024)} %param.8) | copy-start | bytes 21508
  49.4 14.7 %all-to-all-start = ((bf16[4,16,3584]{2,1,0:T(8,128)(2,1)}), bf16[4,16,3584]{2,1,0:T(8,128)(2,1)S(1)}, u32[]{:S(2)}, u32[]{:S(2)}) async-start(bf16[4,16,3584]{2,1,0:T(8,128)(2,1)} %bitcast.7), calls=%async_computation | async-start | bytes 917504 | tf_op jit(solution)/shard_map/all_to_all | solution.py:124
  53.6 74.4 %collective-permute-start.1 = (bf16[512,512]{1,0:T(8,128)(2,1)S(1)}, bf16[512,512]{1,0:T(8,128)(2,1)}, u32[]{:S(2)}, u32[]{:S(2)}) collective-permute-start(bf16[512,512]{1,0:T(8,128)(2,1)S(1)} %all_gather.12.x0_ref), channel_id=1, source_target_pairs={{0,1},{1,2},{2,3},{3,0},{4,5},{5,6},{6,7},{7,4},{8,9},{9,10},{10,1... | collective-permute-start | bytes 1572872 | tf_op jit(solution)/shard_map/ppermute | solution.py:107
  56.7 71.3 %collective-permute-start.2 = (bf16[512,512]{1,0:T(8,128)(2,1)S(1)}, bf16[512,512]{1,0:T(8,128)(2,1)}, u32[]{:S(2)}, u32[]{:S(2)}) collective-permute-start(bf16[512,512]{1,0:T(8,128)(2,1)S(1)} %all_gather.12.x0_ref), channel_id=1, source_target_pairs={{0,2},{1,3},{2,0},{3,1},{4,6},{5,7},{6,4},{7,5},{8,10},{9,11},{10,... | collective-permute-start | bytes 1572872 | tf_op jit(solution)/shard_map/ppermute | solution.py:107
  61.1 66.9 %collective-permute-start.3 = (bf16[512,512]{1,0:T(8,128)(2,1)S(1)}, bf16[512,512]{1,0:T(8,128)(2,1)}, u32[]{:S(2)}, u32[]{:S(2)}) collective-permute-start(bf16[512,512]{1,0:T(8,128)(2,1)S(1)} %all_gather.12.x0_ref), channel_id=1, source_target_pairs={{0,3},{1,0},{2,1},{3,2},{4,7},{5,4},{6,5},{7,6},{8,11},{9,8},{10,9... | collective-permute-start | bytes 1572872 | tf_op jit(solution)/shard_map/ppermute | solution.py:107
  81.3 20.8 %all-to-all-start.2 = ((bf16[8,24,448]{2,1,0:T(8,128)(2,1)}), bf16[8,24,448]{2,1,0:T(8,128)(2,1)S(1)}, u32[]{:S(2)}, u32[]{:S(2)}) async-start(bf16[8,24,448]{2,1,0:T(8,128)(2,1)} %copy.11), calls=%async_computation.2 | async-start | bytes 393216 | tf_op jit(solution)/shard_map/all_to_all | solution.py:139
  87.4 1.5 %copy-start.2 = (bf16[1792,512]{1,0:T(8,128)(2,1)S(1)}, bf16[1792,512]{1,0:T(8,128)(2,1)}, u32[]{:S(2)}) copy-start(bf16[1792,512]{1,0:T(8,128)(2,1)} %param.9) | copy-start | bytes 5505028
  102.2 30.5 %all-to-all-start.1 = ((bf16[8,16,1024]{2,1,0:T(8,128)(2,1)}), bf16[8,16,1024]{2,1,0:T(8,128)(2,1)S(1)}, u32[]{:S(2)}, u32[]{:S(2)}) async-start(bf16[8,16,1024]{2,1,0:T(8,128)(2,1)} %bitcast.8), calls=%async_computation.1 | async-start | bytes 524288 | tf_op jit(solution)/shard_map/all_to_all | solution.py:145
where the time goes:
time: 134 us; the launch traced here: 133 us
  blocking collectives  63.3 us (47%)
  starting transfers between devices  40.4 us (30%)
  waiting for transfers between devices  13.1 us (10%)
  matrix products  5.01 us (4%)
  other arithmetic  4.81 us (4%)
  Pallas kernels  3.31 us (2%)
  local copies, waits for them, and re-layouts  2.56 us (2%)
    all_gather x1, blocking collectives, step(): zall = lax.all_gather(both, ('zh', 'zq', 'zp'), axis=0, tiled=True)  31.8 us
    all_gather x1, blocking collectives, step(): wall = lax.all_gather(wsend, ('y', 'core'), axis=0, tiled=False)  15.8 us
    all_gather x1, blocking collectives, step(): rows = lax.all_gather(hid, ('y', 'core'), axis=0, tiled=True)  15.7 us
    all_to_all x1, waiting for transfers between devices, step(): got = lax.all_to_all(send, ('zh', 'x'), 0, 0)  12.2 us
    ppermute x3, starting transfers between devices, step(): lax.ppermute(zall, 'x', [(i, (i + k) % x_n) for i in range(x_n)])  10.5 us
    ppermute x1, starting transfers between devices, step(): from_core = lax.ppermute(first_products(1 - my_core), 'core', swap)  10.3 us
    all_to_all x1, starting transfers between devices, step(): lax.all_to_all(outs.reshape(2 * y_n, tile, 2 * d_loc), ('zq', 'zp'), 0, 0)  9.33 us
    all_to_all x1, starting transfers between devices, step(): got = lax.all_to_all(send, ('zh', 'x'), 0, 0)  6.05 us
  transfers between devices with their start and end apart: 7, of which 2 were waited for; matrix products, arithmetic and copies ran while one was open for 5% of the time, Pallas kernels for 2%

commit v1 on v0

--- a/solution.py
+++ b/solution.py
@@ -71,6 +71,28 @@
     wout_ref[...] = acc_out.astype(bf16)
 
 
+def in_vmem(x):
+    return pltpu.with_memory_space_constraint(x, pltpu.VMEM)
+
+
+def final_body(parts_ref, first_ref, second_ref):
+    n, _, wide = parts_ref.shape
+    total = parts_ref[0].astype(f32)
+    for j in range(1, n):
+        total = total + parts_ref[j].astype(f32)
+    first_ref[...] = total[:, : wide // 2].astype(bf16)
+    second_ref[...] = total[:, wide // 2 :].astype(bf16)
+
+
+def final_stage(parts):
+    _, tile, wide = parts.shape
+    vmem = pl.BlockSpec(memory_space=pltpu.VMEM)
+    half = jax.ShapeDtypeStruct((tile, wide // 2), bf16)
+    return pl.pallas_call(
+        final_body, in_specs=[vmem], out_specs=(vmem, vmem), out_shape=(half, half), name="final_stage"
+    )(in_vmem(parts))
+
+
 def weight_stage(place, chunks, hid, dep_n):
     _, _, wide = hid.shape
     d_loc = chunks[0].shape[-1]
@@ -86,7 +108,7 @@
         ),
         scratch_shapes=[pltpu.VMEM((len(chunks), chunks[0].shape[0] // 2, wide), bf16)],
         name="weight_stage",
-    )(place, *chunks, hid)
+    )(place, *[in_vmem(c) for c in chunks], in_vmem(hid))
 
 
 def step(tokens, out_grad, w_in, b_in, w_out):
@@ -143,10 +165,7 @@
         axis=1,
     )
     outs = lax.all_to_all(outs.reshape(2 * y_n, tile, 2 * d_loc), ("zq", "zp"), 0, 0)
-    total = outs[0].astype(f32)
-    for j in range(1, 2 * y_n):
-        total = total + outs[j].astype(f32)
-    block_out, tokens_grad = total[:, :d_loc].astype(bf16), total[:, d_loc:].astype(bf16)
+    block_out, tokens_grad = final_stage(outs)
 
     b_sum = jnp.sum(got[:, tile : tile + half].astype(f32) + got[:, tile + half :].astype(f32), axis=0)
     b_pair = jnp.concatenate(hi_lo(b_sum), axis=0)

time: 134 us -> 131 us (0.978)
  matrix products: 5.01 us -> 6.61 us
  local copies, waits for them, and re-layouts: 2.56 us -> 1.17 us
    dot_general x3, matrix products: 3.72 us -> 5.32 us  [dot_nt(): lax.dot_general(a, b, (((1,), (1,)), ((), ())), preferred_element_type=f32)]
  transfers between devices with their start and end apart: 7 -> 7, of which waited for: 2 -> 2; matrix products, arithmetic and copies ran while one was open for 5% -> 6% of each run, Pallas kernels for 2% -> 2%
where the time goes in v1:
time: 131 us
  blocking collectives  62.2 us (47%)
  starting transfers between devices  40.4 us (31%)
  waiting for transfers between devices  12.2 us (9%)
  matrix products  6.61 us (5%)
  other arithmetic  4.64 us (4%)
  Pallas kernels  2.72 us (2%)
    all_gather x1, blocking collectives, step(): zall = lax.all_gather(both, ('zh', 'zq', 'zp'), axis=0, tiled=True)  31.8 us
    all_gather x1, blocking collectives, step(): rows = lax.all_gather(hid, ('y', 'core'), axis=0, tiled=True)  15.7 us
    all_gather x1, blocking collectives, step(): wall = lax.all_gather(wsend, ('y', 'core'), axis=0, tiled=False)  14.7 us
    all_to_all x1, waiting for transfers between devices, step(): got = lax.all_to_all(send, ('zh', 'x'), 0, 0)  11.3 us
    ppermute x3, starting transfers between devices, step(): lax.ppermute(zall, 'x', [(i, (i + k) % x_n) for i in range(x_n)])  10.5 us
    ppermute x1, starting transfers between devices, step(): from_core = lax.ppermute(first_products(1 - my_core), 'core', swap)  10.3 us
    all_to_all x1, starting transfers between devices, step(): lax.all_to_all(outs.reshape(2 * y_n, tile, 2 * d_loc), ('zq', 'zp'), 0, 0)  9.33 us
    all_to_all x1, starting transfers between devices, step(): got = lax.all_to_all(send, ('zh', 'x'), 0, 0)  6.13 us
  transfers between devices with their start and end apart: 7, of which 2 were waited for; matrix products, arithmetic and copies ran while one was open for 6% of the time, Pallas kernels for 2%

profile of v1, /device:TPU:1, one launch (start us, length us, event | category | flops | bytes accessed | tf_op | source)
XLA Modules:
  0.0 130.9 jit_solution(4264135356658007496)
XLA Ops:
  0.6 0.7 pad_maximum_fusion.5
  1.4 31.8 %all_gather.12.x0_ref = bf16[512,512]{1,0:T(8,128)(2,1)S(1)} all-gather(bf16[32,512]{1,0:T(8,128)(2,1)S(1)} %pad_maximum_fusion.5), channel_id=1, replica_groups=mesh['y'=4,'core'=2,'zq'=4,'zp'=2,'zh'=2,'x'=4] {'zh','zq','zp'}, dimensions={0}, use_global_device_ids=true | all-gather | bytes 557056 | tf_op jit(solution)/shard_map/all_gather | solution.py:126
  33.2 0.0 copy-start
  33.2 2.3 %fusion.16 = f32[64,1792]{1,0:T(8,128)S(1)} fusion(bf16[64,512]{1,0:T(8,128)(2,1)S(1)} %bitcast.36, bf16[1792,512]{1,0:T(8,128)(2,1)} %param.9), kind=kOutput, calls=%fused_computation.36 | convolution fusion | flops 117440512 | bytes 2359296 | tf_op jit(solution)/shard_map/dot_general | solution.py:28
  35.5 0.0 copy-done
  35.5 0.0 copy-start.1
  35.5 0.4 fusion.15
  36.0 0.1 pad_maximum_fusion
  36.0 10.3 %collective-permute-start = (f32[64,3584]{1,0:T(8,128)S(1)}, f32[64,3584]{1,0:T(8,128)S(1)}, u32[]{:S(2)}, u32[]{:S(2)}) collective-permute-start(f32[64,3584]{1,0:T(8,128)S(1)} %pad_maximum_fusion), channel_id=1, source_target_pairs={{0,64},{64,0},{1,65},{65,1},{2,66},{66,2},{3,67},{67,3},{4,68},{68... | collective-permute-start | bytes 2752520 | tf_op jit(solution)/shard_map/ppermute | solution.py:144
  46.3 0.0 copy-done.1
  46.3 0.7 fusion.14
  47.0 0.4 fusion.13
  47.4 0.0 copy-start.3
  47.5 0.9 collective-permute-done
  48.4 0.8 fusion
  49.2 4.2 %all-to-all-start = ((bf16[4,16,3584]{2,1,0:T(8,128)(2,1)}), bf16[4,16,3584]{2,1,0:T(8,128)(2,1)S(1)}, u32[]{:S(2)}, u32[]{:S(2)}) async-start(bf16[4,16,3584]{2,1,0:T(8,128)(2,1)} %bitcast.7), calls=%async_computation | async-start | bytes 917504 | tf_op jit(solution)/shard_map/all_to_all | solution.py:146
  53.4 3.1 %collective-permute-start.1 = (bf16[512,512]{1,0:T(8,128)(2,1)S(1)}, bf16[512,512]{1,0:T(8,128)(2,1)S(1)}, u32[]{:S(2)}, u32[]{:S(2)}) collective-permute-start(bf16[512,512]{1,0:T(8,128)(2,1)S(1)} %all_gather.12.x0_ref), channel_id=1, source_target_pairs={{0,1},{1,2},{2,3},{3,0},{4,5},{5,6},{6,7},{7,4},{8,9},{9,10},{10,1... | collective-permute-start | bytes 1572872 | tf_op jit(solution)/shard_map/ppermute | solution.py:129
  56.5 4.4 %collective-permute-start.2 = (bf16[512,512]{1,0:T(8,128)(2,1)S(1)}, bf16[512,512]{1,0:T(8,128)(2,1)S(1)}, u32[]{:S(2)}, u32[]{:S(2)}) collective-permute-start(bf16[512,512]{1,0:T(8,128)(2,1)S(1)} %all_gather.12.x0_ref), channel_id=1, source_target_pairs={{0,2},{1,3},{2,0},{3,1},{4,6},{5,7},{6,4},{7,5},{8,10},{9,11},{10,... | collective-permute-start | bytes 1572872 | tf_op jit(solution)/shard_map/ppermute | solution.py:129
  60.9 3.1 %collective-permute-start.3 = (bf16[512,512]{1,0:T(8,128)(2,1)S(1)}, bf16[512,512]{1,0:T(8,128)(2,1)S(1)}, u32[]{:S(2)}, u32[]{:S(2)}) collective-permute-start(bf16[512,512]{1,0:T(8,128)(2,1)S(1)} %all_gather.12.x0_ref), channel_id=1, source_target_pairs={{0,3},{1,0},{2,1},{3,2},{4,7},{5,4},{6,5},{7,6},{8,11},{9,8},{10,9... | collective-permute-start | bytes 1572872 | tf_op jit(solution)/shard_map/ppermute | solution.py:129
  64.0 0.0 all-to-all-done
  64.0 0.1 convert_reduce_fusion
  64.0 0.0 copy-done.3
  64.1 0.1 fusion.9
  64.2 0.1 reshape.43
  64.3 0.1 reshape.42
  64.5 15.7 %all_gather.13 = bf16[128,3584]{1,0:T(8,128)(2,1)S(1)} all-gather(bf16[16,3584]{1,0:T(8,128)(2,1)S(1)} %pad_maximum_fusion.4), channel_id=1, replica_groups=mesh['y'=4,'core'=2,'zq'=4,'zp'=2,'zh'=2,'x'=4] {'y','core'}, dimensions={0}, use_global_device_ids=true | all-gather | bytes 1032192 | tf_op jit(solution)/shard_map/all_gather | solution.py:162
  80.2 0.1 reshape.44
  80.3 0.1 pad_maximum_fusion.2
  80.4 0.7 copy.11
  81.1 6.1 %all-to-all-start.2 = ((bf16[8,24,448]{2,1,0:T(8,128)(2,1)}), bf16[8,24,448]{2,1,0:T(8,128)(2,1)S(1)}, u32[]{:S(2)}, u32[]{:S(2)}) async-start(bf16[8,24,448]{2,1,0:T(8,128)(2,1)} %copy.11), calls=%async_computation.2 | async-start | bytes 393216 | tf_op jit(solution)/shard_map/all_to_all | solution.py:161
  87.3 0.0 copy-start.2
  87.3 2.4 %convolution_convert_fusion = bf16[128,512]{1,0:T(8,128)(2,1)S(1)} fusion(bf16[512,1792]{1,0:T(8,128)(2,1)} %param.7, bf16[128,3584]{1,0:T(8,128)(2,1)S(1)} %all_gather.13), kind=kOutput, calls=%fused_computation | convolution fusion | flops 234946560 | bytes 2424832 | tf_op jit(solution)/shard_map/dot_general | solution.py:28
  89.6 0.0 copy-done.2
  89.7 0.4 convolution_convert_fusion.1
  90.1 0.7 pad_maximum_fusion.1
  90.8 11.3 %all-to-all-done.2 = bf16[8,24,448]{2,1,0:T(8,128)(2,1)S(1)} async-done(((bf16[8,24,448]{2,1,0:T(8,128)(2,1)}), bf16[8,24,448]{2,1,0:T(8,128)(2,1)S(1)}, u32[]{:S(2)}, u32[]{:S(2)}) %all-to-all-start.2) | async-done | bytes 172064 | tf_op jit(solution)/shard_map/all_to_all | solution.py:161
  102.1 9.3 %all-to-all-start.1 = ((bf16[8,16,1024]{2,1,0:T(8,128)(2,1)}), bf16[8,16,1024]{2,1,0:T(8,128)(2,1)S(1)}, u32[]{:S(2)}, u32[]{:S(2)}) async-start(bf16[8,16,1024]{2,1,0:T(8,128)(2,1)} %bitcast.8), calls=%async_computation.1 | async-start | bytes 524288 | tf_op jit(solution)/shard_map/all_to_all | solution.py:167
  111.4 0.6 pad_add_fusion.place_ref
  112.1 14.7 %all-gather = bf16[1088,448]{1,0:T(8,128)(2,1)S(1)} all-gather(bf16[136,448]{1,0:T(8,128)(2,1)S(1)} %pad_maximum_fusion.3), channel_id=2, replica_groups=mesh['y'=4,'core'=2,'zq'=4,'zp'=2,'zh'=2,'x'=4] {'y','core'}, dimensions={0}, use_global_device_ids=true | all-gather | bytes 1096704 | tf_op jit(solution)/shard_map/all_gather | solution.py:173
  126.8 0.0 collective-permute-done.1.x1_ref
  126.8 0.0 collective-permute-done.2.x2_ref
  126.8 0.0 collective-permute-done.3.x3_ref
  126.8 2.1 %weight_stage.1 = (bf16[224,512]{1,0:T(8,128)(2,1)}, bf16[224,512]{1,0:T(8,128)(2,1)}, f32[1,1792]{1,0:T(1,128)}) custom-call(s32[2]{0:T(128)} %pad_add_fusion.place_ref, bf16[512,512]{1,0:T(8,128)(2,1)S(1)} %all_gather.12.x0_ref, bf16[512,512]{1,0:T(8,128)(2,1)S(1)} %collective-permute-done.1.x1_ref, bf16[512,512]{1,0:T(8,128)(2,1)S(1)} %collective-permute-done.2.x2_ref, ...), custom_call_target="tpu_custom_call" | custom-call | tf_op jit(solution)/shard_map/weight_stage/pallas_call | solution.py:100
  128.9 1.3 %reduce = f32[1792]{0:T(1024)} reduce(f32[1,1792]{1,0:T(1,128)} %get-tuple-element.14, f32[]{:T(128)} %constant.99), dimensions={0}, to_apply=%get-tuple-element.14.reduce_sub_computation | reduce | bytes 14340 | tf_op jit(solution)/shard_map/weight_stage/pallas_call | solution.py:100
  130.2 0.0 all-to-all-done.1.parts_ref
  130.2 0.6 final_stage.1
  (10 shorter events, 0.2 us)
Async XLA Ops:
  33.2 2.3 %copy-start = (bf16[512,1792]{1,0:T(8,128)(2,1)S(1)}, bf16[512,1792]{1,0:T(8,128)(2,1)}, u32[]{:S(2)}) copy-start(bf16[512,1792]{1,0:T(8,128)(2,1)} %param.7) | copy-start | bytes 5505028
  35.5 10.8 %copy-start.1 = (bf16[1792,512]{1,0:T(8,128)(2,1)S(1)}, bf16[1792,512]{1,0:T(8,128)(2,1)}, u32[]{:S(2)}) copy-start(bf16[1792,512]{1,0:T(8,128)(2,1)} %param.9) | copy-start | bytes 5505028
  36.0 12.4 %collective-permute-start = (f32[64,3584]{1,0:T(8,128)S(1)}, f32[64,3584]{1,0:T(8,128)S(1)}, u32[]{:S(2)}, u32[]{:S(2)}) collective-permute-start(f32[64,3584]{1,0:T(8,128)S(1)} %pad_maximum_fusion), channel_id=1, source_target_pairs={{0,64},{64,0},{1,65},{65,1},{2,66},{66,2},{3,67},{67,3},{4,68},{68... | collective-permute-start | bytes 2752520 | tf_op jit(solution)/shard_map/ppermute | solution.py:144
  47.4 16.6 %copy-start.3 = (f32[1792]{0:T(1024)S(1)}, f32[1792]{0:T(1024)}, u32[]{:S(2)}) copy-start(f32[1792]{0:T(1024)} %param.8) | copy-start | bytes 21508
  49.2 14.7 %all-to-all-start = ((bf16[4,16,3584]{2,1,0:T(8,128)(2,1)}), bf16[4,16,3584]{2,1,0:T(8,128)(2,1)S(1)}, u32[]{:S(2)}, u32[]{:S(2)}) async-start(bf16[4,16,3584]{2,1,0:T(8,128)(2,1)} %bitcast.7), calls=%async_computation | async-start | bytes 917504 | tf_op jit(solution)/shard_map/all_to_all | solution.py:146
  53.4 73.4 %collective-permute-start.1 = (bf16[512,512]{1,0:T(8,128)(2,1)S(1)}, bf16[512,512]{1,0:T(8,128)(2,1)S(1)}, u32[]{:S(2)}, u32[]{:S(2)}) collective-permute-start(bf16[512,512]{1,0:T(8,128)(2,1)S(1)} %all_gather.12.x0_ref), channel_id=1, source_target_pairs={{0,1},{1,2},{2,3},{3,0},{4,5},{5,6},{6,7},{7,4},{8,9},{9,10},{10,1... | collective-permute-start | bytes 1572872 | tf_op jit(solution)/shard_map/ppermute | solution.py:129
  56.5 70.3 %collective-permute-start.2 = (bf16[512,512]{1,0:T(8,128)(2,1)S(1)}, bf16[512,512]{1,0:T(8,128)(2,1)S(1)}, u32[]{:S(2)}, u32[]{:S(2)}) collective-permute-start(bf16[512,512]{1,0:T(8,128)(2,1)S(1)} %all_gather.12.x0_ref), channel_id=1, source_target_pairs={{0,2},{1,3},{2,0},{3,1},{4,6},{5,7},{6,4},{7,5},{8,10},{9,11},{10,... | collective-permute-start | bytes 1572872 | tf_op jit(solution)/shard_map/ppermute | solution.py:129
  60.9 65.9 %collective-permute-start.3 = (bf16[512,512]{1,0:T(8,128)(2,1)S(1)}, bf16[512,512]{1,0:T(8,128)(2,1)S(1)}, u32[]{:S(2)}, u32[]{:S(2)}) collective-permute-start(bf16[512,512]{1,0:T(8,128)(2,1)S(1)} %all_gather.12.x0_ref), channel_id=1, source_target_pairs={{0,3},{1,0},{2,1},{3,2},{4,7},{5,4},{6,5},{7,6},{8,11},{9,8},{10,9... | collective-permute-start | bytes 1572872 | tf_op jit(solution)/shard_map/ppermute | solution.py:129
  81.1 20.9 %all-to-all-start.2 = ((bf16[8,24,448]{2,1,0:T(8,128)(2,1)}), bf16[8,24,448]{2,1,0:T(8,128)(2,1)S(1)}, u32[]{:S(2)}, u32[]{:S(2)}) async-start(bf16[8,24,448]{2,1,0:T(8,128)(2,1)} %copy.11), calls=%async_computation.2 | async-start | bytes 393216 | tf_op jit(solution)/shard_map/all_to_all | solution.py:161
  87.3 2.4 %copy-start.2 = (bf16[1792,512]{1,0:T(8,128)(2,1)S(1)}, bf16[1792,512]{1,0:T(8,128)(2,1)}, u32[]{:S(2)}) copy-start(bf16[1792,512]{1,0:T(8,128)(2,1)} %param.9) | copy-start | bytes 5505028
  102.1 28.2 %all-to-all-start.1 = ((bf16[8,16,1024]{2,1,0:T(8,128)(2,1)}), bf16[8,16,1024]{2,1,0:T(8,128)(2,1)S(1)}, u32[]{:S(2)}, u32[]{:S(2)}) async-start(bf16[8,16,1024]{2,1,0:T(8,128)(2,1)} %bitcast.8), calls=%async_computation.1 | async-start | bytes 524288 | tf_op jit(solution)/shard_map/all_to_all | solution.py:167

commit v2 on v1

--- a/solution.py
+++ b/solution.py
@@ -37,22 +37,27 @@
     return hi, (v - hi.astype(f32)).astype(bf16)
 
 
-def weight_body(place_ref, x0_ref, x1_ref, x2_ref, x3_ref, hid_ref, win_ref, wout_ref, b_ref, h_ref):
+def weight_body(x0_ref, x1_ref, x2_ref, x3_ref, hid_ref, win_ref, wout_ref, b_ref, flat_ref, h_ref, x_buf, sem):
     col_n, tall, wide = hid_ref.shape
     part = wide // 2
-    half = b_ref.shape[1] // wide
+    half = flat_ref.shape[1] // wide
     dep_n = 2 * half
     tile = (tall - dep_n) // dep_n
     x_refs = (x0_ref, x1_ref, x2_ref, x3_ref)
     x_n = len(x_refs)
     zh_n = dep_n // x_n
-    my_x = place_ref[1]
+    my_x = lax.axis_index("x")
+    loads = [pltpu.make_async_copy(x_ref, x_buf.at[k], sem.at[k]) for k, x_ref in enumerate(x_refs)]
+    for load in loads:
+        load.start()
     total = jnp.zeros((dep_n, wide), f32)
     for j in range(col_n):
         total = total + hid_ref[j, dep_n * tile :].astype(f32)
     total = total[:half] + total[half:]
     for j in range(half):
-        b_ref[:, j * wide : (j + 1) * wide] = total[j : j + 1]
+        flat_ref[:, j * wide : (j + 1) * wide] = total[j : j + 1]
+    for j in range(b_ref.shape[0]):
+        b_ref[j : j + 1, :] = flat_ref[:, j * 128 : (j + 1) * 128]
     acc_in = jnp.zeros(win_ref.shape, f32)
     acc_out = jnp.zeros(wout_ref.shape, f32)
     for k, x_ref in enumerate(x_refs):
@@ -63,7 +68,8 @@
                 to = (zh * col_n + j) * tile
                 h_ref[k, to : to + tile, :] = hid_ref[j, pl.ds(at, tile), :]
         turned = h_ref[k].T
-        blk = x_ref[...].reshape(-1, 2, tile, x_ref.shape[-1])
+        loads[k].wait()
+        blk = x_buf[k].reshape(-1, 2, tile, x_ref.shape[-1])
         rows = blk.shape[0] * tile
         acc_out += dot_nn(turned[:part], blk[:, 1].reshape(rows, -1))
         acc_in += dot_nn(turned[part:], blk[:, 0].reshape(rows, -1))
@@ -89,26 +95,31 @@
     vmem = pl.BlockSpec(memory_space=pltpu.VMEM)
     half = jax.ShapeDtypeStruct((tile, wide // 2), bf16)
     return pl.pallas_call(
-        final_body, in_specs=[vmem], out_specs=(vmem, vmem), out_shape=(half, half), name="final_stage"
+        final_body, in_specs=[vmem], out_specs=(vmem, vmem), out_shape=(half, half), compiler_params=pltpu.CompilerParams(vmem_limit_bytes=4 << 20), name="final_stage"
     )(in_vmem(parts))
 
 
-def weight_stage(place, chunks, hid, dep_n):
+def weight_stage(chunks, hid, dep_n):
     _, _, wide = hid.shape
     d_loc = chunks[0].shape[-1]
     vmem = pl.BlockSpec(memory_space=pltpu.VMEM)
     return pl.pallas_call(
         weight_body,
-        in_specs=[pl.BlockSpec(memory_space=pltpu.SMEM)] + [vmem] * 5,
+        in_specs=[pl.BlockSpec(memory_space=pl.ANY)] * 4 + [vmem],
         out_specs=(vmem, vmem, vmem),
         out_shape=(
             jax.ShapeDtypeStruct((wide // 2, d_loc), bf16),
             jax.ShapeDtypeStruct((wide // 2, d_loc), bf16),
-            jax.ShapeDtypeStruct((1, wide * dep_n // 2), f32),
+            jax.ShapeDtypeStruct((wide * dep_n // 256, 128), f32),
         ),
-        scratch_shapes=[pltpu.VMEM((len(chunks), chunks[0].shape[0] // 2, wide), bf16)],
-        name="weight_stage",
-    )(place, *[in_vmem(c) for c in chunks], in_vmem(hid))
+        scratch_shapes=[
+            pltpu.VMEM((1, wide * dep_n // 2), f32),
+            pltpu.VMEM((len(chunks), chunks[0].shape[0] // 2, wide), bf16),
+            pltpu.VMEM((len(chunks),) + chunks[0].shape, bf16),
+            pltpu.SemaphoreType.DMA((len(chunks),)),
+        ],
+        compiler_params=pltpu.CompilerParams(vmem_limit_bytes=16 << 20), name="weight_stage",
+    )(*chunks, in_vmem(hid))
 
 
 def step(tokens, out_grad, w_in, b_in, w_out):
@@ -119,7 +130,7 @@
     tile, d_loc = tokens.shape
     f_loc = w_in.shape[1]
     part = f_loc // dep_n
-    my_core, my_x = lax.axis_index("core"), lax.axis_index("x")
+    my_core = lax.axis_index("core")
     swap = [(0, 1), (1, 0)]
 
     both = jnp.concatenate([tokens, out_grad], axis=0)
@@ -171,8 +182,7 @@
     b_pair = jnp.concatenate(hi_lo(b_sum), axis=0)
     wsend = jnp.concatenate([got[:, :tile].reshape(dep_n * tile, 2 * part), b_pair], axis=0)
     wall = lax.all_gather(wsend, ("y", "core"), axis=0, tiled=False)
-    place = jnp.stack([my_core, my_x])
-    w_in_grad, w_out_grad, b_in_grad = weight_stage(place, [zall] + others, wall, dep_n)
+    w_in_grad, w_out_grad, b_in_grad = weight_stage([zall] + others, wall, dep_n)
     return (block_out, tokens_grad, w_in_grad.T, w_out_grad, b_in_grad.reshape(f_loc))
 
 

time: 131 us -> 143 us (1.092)
  the two profiles are of different devices: /device:TPU:1 before, /device:TPU:7 now
where the time goes in v2:
time: 143 us; the launch traced here: 142 us
  blocking collectives  75.1 us (53%)
  starting transfers between devices  36.2 us (25%)
  waiting for transfers between devices  18.4 us (13%)
  matrix products  4.86 us (3%)
  Pallas kernels  2.58 us (2%)
  other arithmetic  2.13 us (1%)
  local copies, waits for them, and re-layouts  1.95 us (1%)
    all_gather x1, blocking collectives, step(): zall = lax.all_gather(both, ('zh', 'zq', 'zp'), axis=0, tiled=True)  31 us
    all_gather x1, blocking collectives, step(): wall = lax.all_gather(wsend, ('y', 'core'), axis=0, tiled=False)  17 us
    all_gather x1, blocking collectives, step(): rows = lax.all_gather(hid, ('y', 'core'), axis=0, tiled=True)  15 us
    all_to_all x1, blocking collectives, step(): pre = lax.all_to_all(pre.reshape(y_n, tile, 2 * f_loc), 'y', 0, 0)  12.2 us
    all_to_all x1, waiting for transfers between devices, step(): got = lax.all_to_all(send, ('zh', 'x'), 0, 0)  10.5 us
    ppermute x1, starting transfers between devices, step(): from_core = lax.ppermute(first_products(1 - my_core), 'core', swap)  10.3 us
    all_to_all x1, starting transfers between devices, step(): lax.all_to_all(outs.reshape(2 * y_n, tile, 2 * d_loc), ('zq', 'zp'), 0, 0)  9.1 us
    all_to_all x1, starting transfers between devices, step(): got = lax.all_to_all(send, ('zh', 'x'), 0, 0)  8.65 us
  transfers between devices with their start and end apart: 6, of which 3 were waited for; matrix products, arithmetic and copies ran while one was open for 2% of the time, Pallas kernels for 1%

profile of v2, /device:TPU:7, one launch (start us, length us, event | category | flops | bytes accessed | tf_op | source)
XLA Modules:
  0.0 142.1 jit_solution(7738261545226974185)
XLA Ops:
  0.6 0.0 copy-start
  0.7 0.9 pad_maximum_fusion.5
  1.5 31.0 %all_gather.12.x0_ref = bf16[512,512]{1,0:T(8,128)(2,1)S(1)} all-gather(bf16[32,512]{1,0:T(8,128)(2,1)S(1)} %pad_maximum_fusion.5), channel_id=1, replica_groups=mesh['y'=4,'core'=2,'zq'=4,'zp'=2,'zh'=2,'x'=4] {'zh','zq','zp'}, dimensions={0}, use_global_device_ids=true | all-gather | bytes 557056 | tf_op jit(solution)/shard_map/all_gather | solution.py:137
  32.5 2.2 %fusion.16 = f32[64,1792]{1,0:T(8,128)S(1)} fusion(bf16[64,512]{1,0:T(8,128)(2,1)S(1)} %bitcast.36, bf16[1792,512]{1,0:T(8,128)(2,1)} %param.9), kind=kOutput, calls=%fused_computation.35 | convolution fusion | flops 117440512 | bytes 2359296 | tf_op jit(solution)/shard_map/dot_general | solution.py:28
  34.7 0.0 copy-done
  34.7 0.0 copy-start.1
  34.7 0.4 fusion.15
  35.2 0.1 pad_maximum_fusion
  35.2 10.3 %collective-permute-start = (f32[64,3584]{1,0:T(8,128)S(1)}, f32[64,3584]{1,0:T(8,128)S(1)}, u32[]{:S(2)}, u32[]{:S(2)}) collective-permute-start(f32[64,3584]{1,0:T(8,128)S(1)} %pad_maximum_fusion), channel_id=1, source_target_pairs={{0,64},{64,0},{1,65},{65,1},{2,66},{66,2},{3,67},{67,3},{4,68},{68... | collective-permute-start | bytes 2752520 | tf_op jit(solution)/shard_map/ppermute | solution.py:155
  45.5 0.0 copy-done.1
  45.5 0.7 fusion.14
  46.2 0.5 fusion.13
  46.7 0.0 copy-start.3
  46.7 0.9 collective-permute-done
  47.6 0.1 fusion
  47.7 12.2 %all_to_all.15 = bf16[4,16,3584]{2,1,0:T(8,128)(2,1)S(1)} all-to-all(bf16[4,16,3584]{2,1,0:T(8,128)(2,1)S(1)} %bitcast.29), channel_id=1, replica_groups=mesh['y'=4,'core'=2,'zq'=4,'zp'=2,'zh'=2,'x'=4] {'y'}, dimensions={0} | all-to-all | bytes 917504 | tf_op jit(solution)/shard_map/all_to_all | solution.py:157
  59.9 0.1 convert_reduce_fusion
  60.0 0.0 copy-done.3
  60.0 0.1 fusion.9
  60.1 0.1 reshape.43
  60.2 0.1 reshape.42
  60.4 15.0 %all_gather.13 = bf16[128,3584]{1,0:T(8,128)(2,1)S(1)} all-gather(bf16[16,3584]{1,0:T(8,128)(2,1)S(1)} %pad_maximum_fusion.4), channel_id=1, replica_groups=mesh['y'=4,'core'=2,'zq'=4,'zp'=2,'zh'=2,'x'=4] {'y','core'}, dimensions={0}, use_global_device_ids=true | all-gather | bytes 1032192 | tf_op jit(solution)/shard_map/all_gather | solution.py:173
  75.4 0.1 reshape.44
  75.5 0.1 pad_maximum_fusion.2
  75.6 0.7 copy.11
  76.3 8.7 %all-to-all-start.2 = ((bf16[8,24,448]{2,1,0:T(8,128)(2,1)}), bf16[8,24,448]{2,1,0:T(8,128)(2,1)S(1)}, u32[]{:S(2)}, u32[]{:S(2)}) async-start(bf16[8,24,448]{2,1,0:T(8,128)(2,1)} %copy.11), calls=%async_computation.2 | async-start | bytes 393216 | tf_op jit(solution)/shard_map/all_to_all | solution.py:172
  85.0 0.0 copy-start.2
  85.0 0.7 convolution_convert_fusion
  85.7 0.8 copy-done.2
  86.5 0.4 convolution_convert_fusion.1
  86.9 0.7 pad_maximum_fusion.1
  87.6 10.5 %all-to-all-done.2 = bf16[8,24,448]{2,1,0:T(8,128)(2,1)S(1)} async-done(((bf16[8,24,448]{2,1,0:T(8,128)(2,1)}), bf16[8,24,448]{2,1,0:T(8,128)(2,1)S(1)}, u32[]{:S(2)}, u32[]{:S(2)}) %all-to-all-start.2) | async-done | bytes 172064 | tf_op jit(solution)/shard_map/all_to_all | solution.py:172
  98.1 9.1 %all-to-all-start.1 = ((bf16[8,16,1024]{2,1,0:T(8,128)(2,1)}), bf16[8,16,1024]{2,1,0:T(8,128)(2,1)S(1)}, u32[]{:S(2)}, u32[]{:S(2)}) async-start(bf16[8,16,1024]{2,1,0:T(8,128)(2,1)} %bitcast.8), calls=%async_computation.1 | async-start | bytes 524288 | tf_op jit(solution)/shard_map/all_to_all | solution.py:178
  107.2 3.8 %collective-permute-start.1 = (bf16[512,512]{1,0:T(8,128)(2,1)S(1)}, bf16[512,512]{1,0:T(8,128)(2,1)S(1)}, u32[]{:S(2)}, u32[]{:S(2)}) collective-permute-start(bf16[512,512]{1,0:T(8,128)(2,1)S(1)} %all_gather.12.x0_ref), channel_id=1, source_target_pairs={{0,1},{1,2},{2,3},{3,0},{4,5},{5,6},{6,7},{7,4},{8,9},{9,10},{10,1... | collective-permute-start | bytes 1572872 | tf_op jit(solution)/shard_map/ppermute | solution.py:140
  111.0 2.4 %collective-permute-start.2 = (bf16[512,512]{1,0:T(8,128)(2,1)S(1)}, bf16[512,512]{1,0:T(8,128)(2,1)S(1)}, u32[]{:S(2)}, u32[]{:S(2)}) collective-permute-start(bf16[512,512]{1,0:T(8,128)(2,1)S(1)} %all_gather.12.x0_ref), channel_id=1, source_target_pairs={{0,2},{1,3},{2,0},{3,1},{4,6},{5,7},{6,4},{7,5},{8,10},{9,11},{10,... | collective-permute-start | bytes 1572872 | tf_op jit(solution)/shard_map/ppermute | solution.py:140
  113.4 2.0 %collective-permute-start.3 = (bf16[512,512]{1,0:T(8,128)(2,1)S(1)}, bf16[512,512]{1,0:T(8,128)(2,1)S(1)}, u32[]{:S(2)}, u32[]{:S(2)}) collective-permute-start(bf16[512,512]{1,0:T(8,128)(2,1)S(1)} %all_gather.12.x0_ref), channel_id=1, source_target_pairs={{0,3},{1,0},{2,1},{3,2},{4,7},{5,4},{6,5},{7,6},{8,11},{9,8},{10,9... | collective-permute-start | bytes 1572872 | tf_op jit(solution)/shard_map/ppermute | solution.py:140
  115.6 17.0 %all-gather = bf16[1088,448]{1,0:T(8,128)(2,1)S(1)} all-gather(bf16[136,448]{1,0:T(8,128)(2,1)S(1)} %pad_maximum_fusion.3), channel_id=2, replica_groups=mesh['y'=4,'core'=2,'zq'=4,'zp'=2,'zh'=2,'x'=4] {'y','core'}, dimensions={0}, use_global_device_ids=true | all-gather | bytes 1096704 | tf_op jit(solution)/shard_map/all_gather | solution.py:184
  132.6 0.0 collective-permute-done.1.x1_ref
  132.6 0.0 collective-permute-done.2.x2_ref
  132.6 6.9 %collective-permute-done.3.x3_ref = bf16[512,512]{1,0:T(8,128)(2,1)S(1)} collective-permute-done((bf16[512,512]{1,0:T(8,128)(2,1)S(1)}, bf16[512,512]{1,0:T(8,128)(2,1)S(1)}, u32[]{:S(2)}, u32[]{:S(2)}) %collective-permute-start.3) | collective-permute-done | bytes 524320 | tf_op jit(solution)/shard_map/ppermute | solution.py:140
  139.5 1.9 %weight_stage.1 = (bf16[224,512]{1,0:T(8,128)(2,1)}, bf16[224,512]{1,0:T(8,128)(2,1)}, f32[14,128]{1,0:T(8,128)}) custom-call(bf16[512,512]{1,0:T(8,128)(2,1)S(1)} %all_gather.12.x0_ref, bf16[512,512]{1,0:T(8,128)(2,1)S(1)} %collective-permute-done.1.x1_ref, bf16[512,512]{1,0:T(8,128)(2,1)S(1)} %collective-permute-done.2.x2_ref, ...), custom_call_target="tpu_custom_call" | custom-call | tf_op jit(solution)/shard_map/weight_stage/pallas_call | solution.py:106
  141.4 0.0 all-to-all-done.1.parts_ref
  141.4 0.6 final_stage.1
  (10 shorter events, 0.2 us)
Async XLA Ops:
  0.6 34.1 %copy-start = (bf16[512,1792]{1,0:T(8,128)(2,1)S(1)}, bf16[512,1792]{1,0:T(8,128)(2,1)}, u32[]{:S(2)}) copy-start(bf16[512,1792]{1,0:T(8,128)(2,1)} %param.7) | copy-start | bytes 5505028
  34.7 10.8 %copy-start.1 = (bf16[1792,512]{1,0:T(8,128)(2,1)S(1)}, bf16[1792,512]{1,0:T(8,128)(2,1)}, u32[]{:S(2)}) copy-start(bf16[1792,512]{1,0:T(8,128)(2,1)} %param.9) | copy-start | bytes 5505028
  35.2 12.4 %collective-permute-start = (f32[64,3584]{1,0:T(8,128)S(1)}, f32[64,3584]{1,0:T(8,128)S(1)}, u32[]{:S(2)}, u32[]{:S(2)}) collective-permute-start(f32[64,3584]{1,0:T(8,128)S(1)} %pad_maximum_fusion), channel_id=1, source_target_pairs={{0,64},{64,0},{1,65},{65,1},{2,66},{66,2},{3,67},{67,3},{4,68},{68... | collective-permute-start | bytes 2752520 | tf_op jit(solution)/shard_map/ppermute | solution.py:155
  46.7 13.3 %copy-start.3 = (f32[1792]{0:T(1024)S(1)}, f32[1792]{0:T(1024)}, u32[]{:S(2)}) copy-start(f32[1792]{0:T(1024)} %param.8) | copy-start | bytes 21508
  76.3 21.8 %all-to-all-start.2 = ((bf16[8,24,448]{2,1,0:T(8,128)(2,1)}), bf16[8,24,448]{2,1,0:T(8,128)(2,1)S(1)}, u32[]{:S(2)}, u32[]{:S(2)}) async-start(bf16[8,24,448]{2,1,0:T(8,128)(2,1)} %copy.11), calls=%async_computation.2 | async-start | bytes 393216 | tf_op jit(solution)/shard_map/all_to_all | solution.py:172
  85.0 1.5 %copy-start.2 = (bf16[1792,512]{1,0:T(8,128)(2,1)S(1)}, bf16[1792,512]{1,0:T(8,128)(2,1)}, u32[]{:S(2)}) copy-start(bf16[1792,512]{1,0:T(8,128)(2,1)} %param.9) | copy-start | bytes 5505028
  98.1 43.3 %all-to-all-start.1 = ((bf16[8,16,1024]{2,1,0:T(8,128)(2,1)}), bf16[8,16,1024]{2,1,0:T(8,128)(2,1)S(1)}, u32[]{:S(2)}, u32[]{:S(2)}) async-start(bf16[8,16,1024]{2,1,0:T(8,128)(2,1)} %bitcast.8), calls=%async_computation.1 | async-start | bytes 524288 | tf_op jit(solution)/shard_map/all_to_all | solution.py:178
  107.2 25.3 %collective-permute-start.1 = (bf16[512,512]{1,0:T(8,128)(2,1)S(1)}, bf16[512,512]{1,0:T(8,128)(2,1)S(1)}, u32[]{:S(2)}, u32[]{:S(2)}) collective-permute-start(bf16[512,512]{1,0:T(8,128)(2,1)S(1)} %all_gather.12.x0_ref), channel_id=1, source_target_pairs={{0,1},{1,2},{2,3},{3,0},{4,5},{5,6},{6,7},{7,4},{8,9},{9,10},{10,1... | collective-permute-start | bytes 1572872 | tf_op jit(solution)/shard_map/ppermute | solution.py:140
  111.0 21.6 %collective-permute-start.2 = (bf16[512,512]{1,0:T(8,128)(2,1)S(1)}, bf16[512,512]{1,0:T(8,128)(2,1)S(1)}, u32[]{:S(2)}, u32[]{:S(2)}) collective-permute-start(bf16[512,512]{1,0:T(8,128)(2,1)S(1)} %all_gather.12.x0_ref), channel_id=1, source_target_pairs={{0,2},{1,3},{2,0},{3,1},{4,6},{5,7},{6,4},{7,5},{8,10},{9,11},{10,... | collective-permute-start | bytes 1572872 | tf_op jit(solution)/shard_map/ppermute | solution.py:140
  113.4 26.1 %collective-permute-start.3 = (bf16[512,512]{1,0:T(8,128)(2,1)S(1)}, bf16[512,512]{1,0:T(8,128)(2,1)S(1)}, u32[]{:S(2)}, u32[]{:S(2)}) collective-permute-start(bf16[512,512]{1,0:T(8,128)(2,1)S(1)} %all_gather.12.x0_ref), channel_id=1, source_target_pairs={{0,3},{1,0},{2,1},{3,2},{4,7},{5,4},{6,5},{7,6},{8,11},{9,8},{10,9... | collective-permute-start | bytes 1572872 | tf_op jit(solution)/shard_map/ppermute | solution.py:140

commit v3 on v2

--- a/solution.py
+++ b/solution.py
@@ -124,37 +124,24 @@
 
 def step(tokens, out_grad, w_in, b_in, w_out):
     y_n, x_n = lax.axis_size("y"), lax.axis_size("x")
-    zh_n = lax.axis_size("zh")
+    zh_n, row_n = lax.axis_size("zh"), y_n * lax.axis_size("core")
     dep_n = zh_n * x_n
     half = dep_n // 2
     tile, d_loc = tokens.shape
     f_loc = w_in.shape[1]
     part = f_loc // dep_n
-    my_core = lax.axis_index("core")
-    swap = [(0, 1), (1, 0)]
-
     both = jnp.concatenate([tokens, out_grad], axis=0)
     zall = lax.all_gather(both, ("zh", "zq", "zp"), axis=0, tiled=True)
     others = []
     for k in range(1, x_n):
         others.append(lax.ppermute(zall, "x", [(i, (i + k) % x_n) for i in range(x_n)]))
     mine = lax.dynamic_index_in_dim(
-        zall.reshape(zh_n, y_n, 2, 2, tile, d_loc), lax.axis_index("zh"), 0, keepdims=False
+        zall.reshape(zh_n, row_n, 2, tile, d_loc), lax.axis_index("zh"), 0, keepdims=False
     )
-
-    def first_products(core):
-        blk = lax.dynamic_index_in_dim(mine, core, 1, keepdims=False)
-        return jnp.concatenate(
-            [
-                dot_nn(blk[:, 0].reshape(y_n * tile, d_loc), w_in),
-                dot_nt(blk[:, 1].reshape(y_n * tile, d_loc), w_out),
-            ],
-            axis=1,
-        )
-
-    from_core = lax.ppermute(first_products(1 - my_core), "core", swap)
-    pre = (first_products(my_core) + from_core).astype(bf16)
-    pre = lax.all_to_all(pre.reshape(y_n, tile, 2 * f_loc), "y", 0, 0)
+    pre_part = dot_nn(mine[:, 0].reshape(row_n * tile, d_loc), w_in).astype(bf16)
+    grad_part = dot_nt(mine[:, 1].reshape(row_n * tile, d_loc), w_out).astype(bf16)
+    pre = jnp.concatenate([pre_part, grad_part], axis=1)
+    pre = lax.all_to_all(pre.reshape(row_n, tile, 2 * f_loc), ("y", "core"), 0, 0)
     pre = jnp.sum(pre.astype(f32), axis=0)
     value, slope = gelu_parts(pre[:, :f_loc] + b_in)
     pre_grad = pre[:, f_loc:] * slope
@@ -175,7 +162,7 @@
         [dot_nn(rows[:, :f_loc], w_out).astype(bf16), dot_nt(rows[:, f_loc:], w_in).astype(bf16)],
         axis=1,
     )
-    outs = lax.all_to_all(outs.reshape(2 * y_n, tile, 2 * d_loc), ("zq", "zp"), 0, 0)
+    outs = lax.all_to_all(outs.reshape(row_n, tile, 2 * d_loc), ("zq", "zp"), 0, 0)
     block_out, tokens_grad = final_stage(outs)
 
     b_sum = jnp.sum(got[:, tile : tile + half].astype(f32) + got[:, tile + half :].astype(f32), axis=0)

time: 143 us -> 130 us (0.909)
  the two profiles are of different devices: /device:TPU:7 before, /device:TPU:481 now
where the time goes in v3:
time: 130 us
  blocking collectives  77.7 us (60%)
  starting transfers between devices  33.7 us (26%)
  waiting for transfers between devices  8.02 us (6%)
  matrix products  3.74 us (3%)
  Pallas kernels  2.59 us (2%)
  other arithmetic  2.11 us (2%)
    all_to_all x1, blocking collectives, step(): lax.all_to_all(pre.reshape(row_n, tile, 2 * f_loc), ('y', 'core'), 0, 0)  25.5 us
    all_gather x1, blocking collectives, step(): zall = lax.all_gather(both, ('zh', 'zq', 'zp'), axis=0, tiled=True)  21.8 us
    all_gather x1, blocking collectives, step(): wall = lax.all_gather(wsend, ('y', 'core'), axis=0, tiled=False)  15.4 us
    all_gather x1, blocking collectives, step(): rows = lax.all_gather(hid, ('y', 'core'), axis=0, tiled=True)  15 us
    all_to_all x1, starting transfers between devices, step(): got = lax.all_to_all(send, ('zh', 'x'), 0, 0)  13.9 us
    all_to_all x1, starting transfers between devices, step(): lax.all_to_all(outs.reshape(row_n, tile, 2 * d_loc), ('zq', 'zp'), 0, 0)  10.5 us
    ppermute x3, starting transfers between devices, step(): lax.ppermute(zall, 'x', [(i, (i + k) % x_n) for i in range(x_n)])  9.27 us
    ppermute x3, waiting for transfers between devices, step(): lax.ppermute(zall, 'x', [(i, (i + k) % x_n) for i in range(x_n)])  8.02 us
  transfers between devices with their start and end apart: 5, of which 1 were waited for; matrix products, arithmetic and copies ran while one was open for 1% of the time, Pallas kernels for 1%

profile of v3, /device:TPU:481, one launch (start us, length us, event | category | flops | bytes accessed | tf_op | source)
XLA Modules:
  0.0 129.9 jit_solution(15959899238752723857)
XLA Ops:
  0.6 0.0 copy-start
  0.7 0.9 pad_maximum_fusion.5
  1.5 21.8 %all_gather.12.x0_ref = bf16[512,512]{1,0:T(8,128)(2,1)S(1)} all-gather(bf16[32,512]{1,0:T(8,128)(2,1)S(1)} %pad_maximum_fusion.5), channel_id=1, replica_groups=mesh['y'=4,'core'=2,'zq'=4,'zp'=2,'zh'=2,'x'=4] {'zh','zq','zp'}, dimensions={0}, use_global_device_ids=true | all-gather | bytes 557056 | tf_op jit(solution)/shard_map/all_gather | solution.py:134
  23.4 2.2 %convolution_convert_fusion = bf16[128,1792]{1,0:T(8,128)(2,1)S(1)} fusion(bf16[128,512]{1,0:T(8,128)(2,1)S(1)} %bitcast.24, bf16[1792,512]{1,0:T(8,128)(2,1)} %param.9), kind=kOutput, calls=%fused_computation | convolution fusion | flops 235110400 | bytes 2424832 | tf_op jit(solution)/shard_map/dot_general | solution.py:28
  25.6 0.0 copy-done
  25.6 0.4 convolution_convert_fusion.1
  26.1 0.1 pad_maximum_fusion
  26.1 0.0 copy-start.2
  26.1 25.5 %all_to_all.15 = bf16[8,16,3584]{2,1,0:T(8,128)(2,1)S(1)} all-to-all(bf16[8,16,3584]{2,1,0:T(8,128)(2,1)S(1)} %bitcast.21), channel_id=1, replica_groups=mesh['y'=4,'core'=2,'zq'=4,'zp'=2,'zh'=2,'x'=4] {'y','core'}, dimensions={0} | all-to-all | bytes 1835008 | tf_op jit(solution)/shard_map/all_to_all | solution.py:144
  51.7 0.1 convert_reduce_fusion
  51.8 0.0 copy-done.2
  51.8 0.1 fusion.8
  52.0 0.1 reshape.39
  52.1 0.1 reshape.38
  52.3 0.1 reshape.40
  52.4 0.1 pad_maximum_fusion.2
  52.5 0.7 copy.11
  53.2 13.9 %all-to-all-start.2 = ((bf16[8,24,448]{2,1,0:T(8,128)(2,1)}), bf16[8,24,448]{2,1,0:T(8,128)(2,1)S(1)}, u32[]{:S(2)}, u32[]{:S(2)}) async-start(bf16[8,24,448]{2,1,0:T(8,128)(2,1)} %copy.11), calls=%async_computation.2 | async-start | bytes 393216 | tf_op jit(solution)/shard_map/all_to_all | solution.py:159
  67.1 0.0 copy-start.1
  67.1 15.0 %all_gather.13 = bf16[128,3584]{1,0:T(8,128)(2,1)S(1)} all-gather(bf16[16,3584]{1,0:T(8,128)(2,1)S(1)} %pad_maximum_fusion.4), channel_id=1, replica_groups=mesh['y'=4,'core'=2,'zq'=4,'zp'=2,'zh'=2,'x'=4] {'y','core'}, dimensions={0}, use_global_device_ids=true | all-gather | bytes 1032192 | tf_op jit(solution)/shard_map/all_gather | solution.py:160
  82.1 0.7 convolution_convert_fusion.2
  82.9 0.0 copy-done.1
  82.9 0.4 convolution_convert_fusion.3
  83.3 0.7 pad_maximum_fusion.1
  84.0 0.0 all-to-all-done.2
  84.0 10.5 %all-to-all-start.1 = ((bf16[8,16,1024]{2,1,0:T(8,128)(2,1)}), bf16[8,16,1024]{2,1,0:T(8,128)(2,1)S(1)}, u32[]{:S(2)}, u32[]{:S(2)}) async-start(bf16[8,16,1024]{2,1,0:T(8,128)(2,1)} %bitcast.5), calls=%async_computation.1 | async-start | bytes 524288 | tf_op jit(solution)/shard_map/all_to_all | solution.py:165
  94.5 4.3 %collective-permute-start.2 = (bf16[512,512]{1,0:T(8,128)(2,1)S(1)}, bf16[512,512]{1,0:T(8,128)(2,1)S(1)}, u32[]{:S(2)}, u32[]{:S(2)}) collective-permute-start(bf16[512,512]{1,0:T(8,128)(2,1)S(1)} %all_gather.12.x0_ref), channel_id=1, source_target_pairs={{0,3},{1,0},{2,1},{3,2},{4,7},{5,4},{6,5},{7,6},{8,11},{9,8},{10,9... | collective-permute-start | bytes 1572872 | tf_op jit(solution)/shard_map/ppermute | solution.py:137
  98.8 2.5 %collective-permute-start.1 = (bf16[512,512]{1,0:T(8,128)(2,1)S(1)}, bf16[512,512]{1,0:T(8,128)(2,1)S(1)}, u32[]{:S(2)}, u32[]{:S(2)}) collective-permute-start(bf16[512,512]{1,0:T(8,128)(2,1)S(1)} %all_gather.12.x0_ref), channel_id=1, source_target_pairs={{0,2},{1,3},{2,0},{3,1},{4,6},{5,7},{6,4},{7,5},{8,10},{9,11},{10,... | collective-permute-start | bytes 1572872 | tf_op jit(solution)/shard_map/ppermute | solution.py:137
  101.3 2.5 %collective-permute-start = (bf16[512,512]{1,0:T(8,128)(2,1)S(1)}, bf16[512,512]{1,0:T(8,128)(2,1)S(1)}, u32[]{:S(2)}, u32[]{:S(2)}) collective-permute-start(bf16[512,512]{1,0:T(8,128)(2,1)S(1)} %all_gather.12.x0_ref), channel_id=1, source_target_pairs={{0,1},{1,2},{2,3},{3,0},{4,5},{5,6},{6,7},{7,4},{8,9},{9,10},{10,1... | collective-permute-start | bytes 1572872 | tf_op jit(solution)/shard_map/ppermute | solution.py:137
  103.9 15.4 %all-gather = bf16[1088,448]{1,0:T(8,128)(2,1)S(1)} all-gather(bf16[136,448]{1,0:T(8,128)(2,1)S(1)} %pad_maximum_fusion.3), channel_id=2, replica_groups=mesh['y'=4,'core'=2,'zq'=4,'zp'=2,'zh'=2,'x'=4] {'y','core'}, dimensions={0}, use_global_device_ids=true | all-gather | bytes 1096704 | tf_op jit(solution)/shard_map/all_gather | solution.py:171
  119.2 0.0 collective-permute-done.2.x3_ref
  119.2 0.0 collective-permute-done.1.x2_ref
  119.2 8.0 %collective-permute-done.x1_ref = bf16[512,512]{1,0:T(8,128)(2,1)S(1)} collective-permute-done((bf16[512,512]{1,0:T(8,128)(2,1)S(1)}, bf16[512,512]{1,0:T(8,128)(2,1)S(1)}, u32[]{:S(2)}, u32[]{:S(2)}) %collective-permute-start) | collective-permute-done | bytes 524320 | tf_op jit(solution)/shard_map/ppermute | solution.py:137
  127.3 1.9 %weight_stage.1 = (bf16[224,512]{1,0:T(8,128)(2,1)}, bf16[224,512]{1,0:T(8,128)(2,1)}, f32[14,128]{1,0:T(8,128)}) custom-call(bf16[512,512]{1,0:T(8,128)(2,1)S(1)} %all_gather.12.x0_ref, bf16[512,512]{1,0:T(8,128)(2,1)S(1)} %collective-permute-done.x1_ref, bf16[512,512]{1,0:T(8,128)(2,1)S(1)} %collective-permute-done.1.x2_ref, ...), custom_call_target="tpu_custom_call" | custom-call | tf_op jit(solution)/shard_map/weight_stage/pallas_call | solution.py:106
  129.2 0.0 all-to-all-done.1.parts_ref
  129.2 0.6 final_stage.1
  (10 shorter events, 0.2 us)
Async XLA Ops:
  0.6 25.0 %copy-start = (bf16[512,1792]{1,0:T(8,128)(2,1)S(1)}, bf16[512,1792]{1,0:T(8,128)(2,1)}, u32[]{:S(2)}) copy-start(bf16[512,1792]{1,0:T(8,128)(2,1)} %param.7) | copy-start | bytes 5505028
  26.1 25.7 %copy-start.2 = (f32[1792]{0:T(1024)S(1)}, f32[1792]{0:T(1024)}, u32[]{:S(2)}) copy-start(f32[1792]{0:T(1024)} %param.8) | copy-start | bytes 21508
  53.2 30.8 %all-to-all-start.2 = ((bf16[8,24,448]{2,1,0:T(8,128)(2,1)}), bf16[8,24,448]{2,1,0:T(8,128)(2,1)S(1)}, u32[]{:S(2)}, u32[]{:S(2)}) async-start(bf16[8,24,448]{2,1,0:T(8,128)(2,1)} %copy.11), calls=%async_computation.2 | async-start | bytes 393216 | tf_op jit(solution)/shard_map/all_to_all | solution.py:159
  67.1 15.7 %copy-start.1 = (bf16[1792,512]{1,0:T(8,128)(2,1)S(1)}, bf16[1792,512]{1,0:T(8,128)(2,1)}, u32[]{:S(2)}) copy-start(bf16[1792,512]{1,0:T(8,128)(2,1)} %param.9) | copy-start | bytes 5505028
  84.0 45.2 %all-to-all-start.1 = ((bf16[8,16,1024]{2,1,0:T(8,128)(2,1)}), bf16[8,16,1024]{2,1,0:T(8,128)(2,1)S(1)}, u32[]{:S(2)}, u32[]{:S(2)}) async-start(bf16[8,16,1024]{2,1,0:T(8,128)(2,1)} %bitcast.5), calls=%async_computation.1 | async-start | bytes 524288 | tf_op jit(solution)/shard_map/all_to_all | solution.py:165
  94.5 24.8 %collective-permute-start.2 = (bf16[512,512]{1,0:T(8,128)(2,1)S(1)}, bf16[512,512]{1,0:T(8,128)(2,1)S(1)}, u32[]{:S(2)}, u32[]{:S(2)}) collective-permute-start(bf16[512,512]{1,0:T(8,128)(2,1)S(1)} %all_gather.12.x0_ref), channel_id=1, source_target_pairs={{0,3},{1,0},{2,1},{3,2},{4,7},{5,4},{6,5},{7,6},{8,11},{9,8},{10,9... | collective-permute-start | bytes 1572872 | tf_op jit(solution)/shard_map/ppermute | solution.py:137
  98.8 20.5 %collective-permute-start.1 = (bf16[512,512]{1,0:T(8,128)(2,1)S(1)}, bf16[512,512]{1,0:T(8,128)(2,1)S(1)}, u32[]{:S(2)}, u32[]{:S(2)}) collective-permute-start(bf16[512,512]{1,0:T(8,128)(2,1)S(1)} %all_gather.12.x0_ref), channel_id=1, source_target_pairs={{0,2},{1,3},{2,0},{3,1},{4,6},{5,7},{6,4},{7,5},{8,10},{9,11},{10,... | collective-permute-start | bytes 1572872 | tf_op jit(solution)/shard_map/ppermute | solution.py:137
  101.3 26.0 %collective-permute-start = (bf16[512,512]{1,0:T(8,128)(2,1)S(1)}, bf16[512,512]{1,0:T(8,128)(2,1)S(1)}, u32[]{:S(2)}, u32[]{:S(2)}) collective-permute-start(bf16[512,512]{1,0:T(8,128)(2,1)S(1)} %all_gather.12.x0_ref), channel_id=1, source_target_pairs={{0,1},{1,2},{2,3},{3,0},{4,5},{5,6},{6,7},{7,4},{8,9},{9,10},{10,1... | collective-permute-start | bytes 1572872 | tf_op jit(solution)/shard_map/ppermute | solution.py:137

commit v4 on v2

--- a/solution.py
+++ b/solution.py
@@ -1,3 +1,5 @@
+import functools
+
 import jax
 import jax.numpy as jnp
 from jax import lax
@@ -35,6 +37,45 @@
 def hi_lo(v):
     hi = v.astype(bf16)
     return hi, (v - hi.astype(f32)).astype(bf16)
+
+
+def gelu_body(dep_n, recv_ref, bias_ref, hid_ref, send_ref):
+    y_n, tile, wide = recv_ref.shape
+    f_loc = wide // 2
+    part = f_loc // dep_n
+    half = dep_n // 2
+    pre = recv_ref[0].astype(f32)
+    for j in range(1, y_n):
+        pre = pre + recv_ref[j].astype(f32)
+    bias = jnp.concatenate([bias_ref[j : j + 1, :] for j in range(bias_ref.shape[0])], axis=1)
+    value, slope = gelu_parts(pre[:, :f_loc] + bias)
+    pre_grad = pre[:, f_loc:] * slope
+    hid_ref[:, :f_loc] = value.astype(bf16)
+    hid_ref[:, f_loc:] = pre_grad.astype(bf16)
+    rows = jnp.sum(pre_grad, axis=0, keepdims=True)
+    high = rows.astype(bf16).astype(f32)
+    extra = [v[:, j * 2 * part : (j + 1) * 2 * part] for v in (high, rows - high) for j in range(half)]
+    extra = jnp.concatenate(extra, axis=0).astype(bf16)
+    for d in range(dep_n):
+        cut = slice(d * part, (d + 1) * part)
+        send_ref[d, :tile] = jnp.concatenate([value[:, cut], pre_grad[:, cut]], axis=1).astype(bf16)
+        send_ref[d, tile:] = extra
+
+
+def gelu_stage(recv, bias, dep_n):
+    _, tile, wide = recv.shape
+    vmem = pl.BlockSpec(memory_space=pltpu.VMEM)
+    return pl.pallas_call(
+        functools.partial(gelu_body, dep_n),
+        in_specs=[vmem, vmem],
+        out_specs=(vmem, vmem),
+        out_shape=(
+            jax.ShapeDtypeStruct((tile, wide), bf16),
+            jax.ShapeDtypeStruct((dep_n, tile + dep_n, wide // dep_n), bf16),
+        ),
+        compiler_params=pltpu.CompilerParams(vmem_limit_bytes=8 << 20),
+        name="gelu_stage",
+    )(in_vmem(recv), bias.reshape(-1, 128))
 
 
 def weight_body(x0_ref, x1_ref, x2_ref, x3_ref, hid_ref, win_ref, wout_ref, b_ref, flat_ref, h_ref, x_buf, sem):
@@ -144,31 +185,14 @@
 
     def first_products(core):
         blk = lax.dynamic_index_in_dim(mine, core, 1, keepdims=False)
-        return jnp.concatenate(
-            [
-                dot_nn(blk[:, 0].reshape(y_n * tile, d_loc), w_in),
-                dot_nt(blk[:, 1].reshape(y_n * tile, d_loc), w_out),
-            ],
-            axis=1,
-        )
+        part_in = dot_nn(blk[:, 0].reshape(y_n * tile, d_loc), w_in)
+        part_out = dot_nt(blk[:, 1].reshape(y_n * tile, d_loc), w_out)
+        return jnp.concatenate([part_in, part_out], axis=1)
 
     from_core = lax.ppermute(first_products(1 - my_core), "core", swap)
     pre = (first_products(my_core) + from_core).astype(bf16)
     pre = lax.all_to_all(pre.reshape(y_n, tile, 2 * f_loc), "y", 0, 0)
-    pre = jnp.sum(pre.astype(f32), axis=0)
-    value, slope = gelu_parts(pre[:, :f_loc] + b_in)
-    pre_grad = pre[:, f_loc:] * slope
-    act, hgrad = value.astype(bf16), pre_grad.astype(bf16)
-    hid = jnp.concatenate([act, hgrad], axis=1)
-    b_rows = jnp.concatenate(hi_lo(jnp.sum(pre_grad, axis=0).reshape(half, 2 * part)), axis=0)
-    send = jnp.concatenate(
-        [
-            act.reshape(tile, dep_n, part).transpose(1, 0, 2),
-            hgrad.reshape(tile, dep_n, part).transpose(1, 0, 2),
-        ],
-        axis=2,
-    )
-    send = jnp.concatenate([send, jnp.broadcast_to(b_rows, (dep_n,) + b_rows.shape)], axis=1)
+    hid, send = gelu_stage(pre, b_in, dep_n)
     got = lax.all_to_all(send, ("zh", "x"), 0, 0)
     rows = lax.all_gather(hid, ("y", "core"), axis=0, tiled=True)
     outs = jnp.concatenate(

time: 143 us -> 142 us (level)
  no operation moved by 1% of the time
where the time goes in v4:
time: 142 us
  blocking collectives  75.1 us (53%)
  starting transfers between devices  36.2 us (25%)
  waiting for transfers between devices  18.4 us (13%)
  matrix products  4.85 us (3%)
  Pallas kernels  3.51 us (2%)
  other arithmetic  1.81 us (1%)
    all_gather x1, blocking collectives, step(): zall = lax.all_gather(both, ('zh', 'zq', 'zp'), axis=0, tiled=True)  31 us
    all_gather x1, blocking collectives, step(): wall = lax.all_gather(wsend, ('y', 'core'), axis=0, tiled=False)  17 us
    all_gather x1, blocking collectives, step(): rows = lax.all_gather(hid, ('y', 'core'), axis=0, tiled=True)  15 us
    all_to_all x1, blocking collectives, step(): pre = lax.all_to_all(pre.reshape(y_n, tile, 2 * f_loc), 'y', 0, 0)  12.2 us
    all_to_all x1, waiting for transfers between devices, step(): got = lax.all_to_all(send, ('zh', 'x'), 0, 0)  10.5 us
    ppermute x1, starting transfers between devices, step(): from_core = lax.ppermute(first_products(1 - my_core), 'core', swap)  10.3 us
    all_to_all x1, starting transfers between devices, step(): lax.all_to_all(outs.reshape(2 * y_n, tile, 2 * d_loc), ('zq', 'zp'), 0, 0)  9.1 us
    all_to_all x1, starting transfers between devices, step(): got = lax.all_to_all(send, ('zh', 'x'), 0, 0)  8.65 us
  transfers between devices with their start and end apart: 6, of which 3 were waited for; matrix products, arithmetic and copies ran while one was open for 2% of the time, Pallas kernels for 1%

profile of v4, /device:TPU:7, one launch (start us, length us, event | category | flops | bytes accessed | tf_op | source)
XLA Modules:
  0.0 141.5 jit_solution(4998435203904839990)
XLA Ops:
  0.6 0.0 copy-start
  0.7 0.9 pad_maximum_fusion.3
  1.5 31.0 %all_gather.12.x0_ref = bf16[512,512]{1,0:T(8,128)(2,1)S(1)} all-gather(bf16[32,512]{1,0:T(8,128)(2,1)S(1)} %pad_maximum_fusion.3), channel_id=1, replica_groups=mesh['y'=4,'core'=2,'zq'=4,'zp'=2,'zh'=2,'x'=4] {'zh','zq','zp'}, dimensions={0}, use_global_device_ids=true | all-gather | bytes 557056 | tf_op jit(solution)/shard_map/all_gather | solution.py:178
  32.5 2.2 %fusion.8 = f32[64,1792]{1,0:T(8,128)S(1)} fusion(bf16[64,512]{1,0:T(8,128)(2,1)S(1)} %bitcast.34, bf16[1792,512]{1,0:T(8,128)(2,1)} %param.9), kind=kOutput, calls=%fused_computation.19 | convolution fusion | flops 117440512 | bytes 2359296 | tf_op jit(solution)/shard_map/dot_general | solution.py:30
  34.7 0.0 copy-done
  34.7 0.0 copy-start.2
  34.7 0.4 fusion.7
  35.2 0.1 pad_maximum_fusion
  35.2 10.3 %collective-permute-start = (f32[64,3584]{1,0:T(8,128)S(1)}, f32[64,3584]{1,0:T(8,128)S(1)}, u32[]{:S(2)}, u32[]{:S(2)}) collective-permute-start(f32[64,3584]{1,0:T(8,128)S(1)} %pad_maximum_fusion), channel_id=1, source_target_pairs={{0,64},{64,0},{1,65},{65,1},{2,66},{66,2},{3,67},{67,3},{4,68},{68... | collective-permute-start | bytes 2752520 | tf_op jit(solution)/shard_map/ppermute | solution.py:192
  45.5 0.0 copy-done.2
  45.5 0.7 fusion.6
  46.2 0.4 fusion.5
  46.6 0.0 copy-start.1
  46.6 0.9 collective-permute-done
  47.6 0.1 fusion
  47.7 12.2 %all_to_all.15.recv_ref = bf16[4,16,3584]{2,1,0:T(8,128)(2,1)S(1)} all-to-all(bf16[4,16,3584]{2,1,0:T(8,128)(2,1)S(1)} %bitcast.29), channel_id=1, replica_groups=mesh['y'=4,'core'=2,'zq'=4,'zp'=2,'zh'=2,'x'=4] {'y'}, dimensions={0} | all-to-all | bytes 917504 | tf_op jit(solution)/shard_map/all_to_all | solution.py:194
  59.9 0.0 copy-done.1
  59.9 0.9 gelu_stage.1
  60.8 15.0 %all_gather.13 = bf16[128,3584]{1,0:T(8,128)(2,1)S(1)} all-gather(bf16[16,3584]{1,0:T(8,128)(2,1)S(1)} %get-tuple-element.12), channel_id=1, replica_groups=mesh['y'=4,'core'=2,'zq'=4,'zp'=2,'zh'=2,'x'=4] {'y','core'}, dimensions={0}, use_global_device_ids=true | all-gather | bytes 1032192 | tf_op jit(solution)/shard_map/all_gather | solution.py:197
  75.8 8.7 %all-to-all-start.2 = ((bf16[8,24,448]{2,1,0:T(8,128)(2,1)}), bf16[8,24,448]{2,1,0:T(8,128)(2,1)S(1)}, u32[]{:S(2)}, u32[]{:S(2)}) async-start(bf16[8,24,448]{2,1,0:T(8,128)(2,1)} %get-tuple-element.15), calls=%async_computation.2 | async-start | bytes 393216 | tf_op jit(solution)/shard_map/all_to_all | solution.py:196
  84.4 0.0 copy-start.3
  84.4 0.7 convolution_convert_fusion
  85.1 0.8 copy-done.3
  85.9 0.4 convolution_convert_fusion.1
  86.3 0.7 pad_maximum_fusion.1
  87.1 10.5 %all-to-all-done.2 = bf16[8,24,448]{2,1,0:T(8,128)(2,1)S(1)} async-done(((bf16[8,24,448]{2,1,0:T(8,128)(2,1)}), bf16[8,24,448]{2,1,0:T(8,128)(2,1)S(1)}, u32[]{:S(2)}, u32[]{:S(2)}) %all-to-all-start.2) | async-done | bytes 172064 | tf_op jit(solution)/shard_map/all_to_all | solution.py:196
  97.6 9.1 %all-to-all-start.1 = ((bf16[8,16,1024]{2,1,0:T(8,128)(2,1)}), bf16[8,16,1024]{2,1,0:T(8,128)(2,1)S(1)}, u32[]{:S(2)}, u32[]{:S(2)}) async-start(bf16[8,16,1024]{2,1,0:T(8,128)(2,1)} %bitcast.9), calls=%async_computation.1 | async-start | bytes 524288 | tf_op jit(solution)/shard_map/all_to_all | solution.py:202
  106.7 3.8 %collective-permute-start.1 = (bf16[512,512]{1,0:T(8,128)(2,1)S(1)}, bf16[512,512]{1,0:T(8,128)(2,1)S(1)}, u32[]{:S(2)}, u32[]{:S(2)}) collective-permute-start(bf16[512,512]{1,0:T(8,128)(2,1)S(1)} %all_gather.12.x0_ref), channel_id=1, source_target_pairs={{0,1},{1,2},{2,3},{3,0},{4,5},{5,6},{6,7},{7,4},{8,9},{9,10},{10,1... | collective-permute-start | bytes 1572872 | tf_op jit(solution)/shard_map/ppermute | solution.py:181
  110.4 2.4 %collective-permute-start.2 = (bf16[512,512]{1,0:T(8,128)(2,1)S(1)}, bf16[512,512]{1,0:T(8,128)(2,1)S(1)}, u32[]{:S(2)}, u32[]{:S(2)}) collective-permute-start(bf16[512,512]{1,0:T(8,128)(2,1)S(1)} %all_gather.12.x0_ref), channel_id=1, source_target_pairs={{0,2},{1,3},{2,0},{3,1},{4,6},{5,7},{6,4},{7,5},{8,10},{9,11},{10,... | collective-permute-start | bytes 1572872 | tf_op jit(solution)/shard_map/ppermute | solution.py:181
  112.9 2.0 %collective-permute-start.3 = (bf16[512,512]{1,0:T(8,128)(2,1)S(1)}, bf16[512,512]{1,0:T(8,128)(2,1)S(1)}, u32[]{:S(2)}, u32[]{:S(2)}) collective-permute-start(bf16[512,512]{1,0:T(8,128)(2,1)S(1)} %all_gather.12.x0_ref), channel_id=1, source_target_pairs={{0,3},{1,0},{2,1},{3,2},{4,7},{5,4},{6,5},{7,6},{8,11},{9,8},{10,9... | collective-permute-start | bytes 1572872 | tf_op jit(solution)/shard_map/ppermute | solution.py:181
  115.0 17.0 %all-gather = bf16[1088,448]{1,0:T(8,128)(2,1)S(1)} all-gather(bf16[136,448]{1,0:T(8,128)(2,1)S(1)} %pad_maximum_fusion.2), channel_id=2, replica_groups=mesh['y'=4,'core'=2,'zq'=4,'zp'=2,'zh'=2,'x'=4] {'y','core'}, dimensions={0}, use_global_device_ids=true | all-gather | bytes 1096704 | tf_op jit(solution)/shard_map/all_gather | solution.py:208
  132.0 0.0 collective-permute-done.1.x1_ref
  132.0 0.0 collective-permute-done.2.x2_ref
  132.0 6.9 %collective-permute-done.3.x3_ref = bf16[512,512]{1,0:T(8,128)(2,1)S(1)} collective-permute-done((bf16[512,512]{1,0:T(8,128)(2,1)S(1)}, bf16[512,512]{1,0:T(8,128)(2,1)S(1)}, u32[]{:S(2)}, u32[]{:S(2)}) %collective-permute-start.3) | collective-permute-done | bytes 524320 | tf_op jit(solution)/shard_map/ppermute | solution.py:181
  138.9 1.9 %weight_stage.1 = (bf16[224,512]{1,0:T(8,128)(2,1)}, bf16[224,512]{1,0:T(8,128)(2,1)}, f32[14,128]{1,0:T(8,128)}) custom-call(bf16[512,512]{1,0:T(8,128)(2,1)S(1)} %all_gather.12.x0_ref, bf16[512,512]{1,0:T(8,128)(2,1)S(1)} %collective-permute-done.1.x1_ref, bf16[512,512]{1,0:T(8,128)(2,1)S(1)} %collective-permute-done.2.x2_ref, ...), custom_call_target="tpu_custom_call" | custom-call | tf_op jit(solution)/shard_map/weight_stage/pallas_call | solution.py:147
  140.9 0.0 all-to-all-done.1.parts_ref
  140.9 0.6 final_stage.1
  (6 shorter events, 0.1 us)
Async XLA Ops:
  0.6 34.1 %copy-start = (bf16[512,1792]{1,0:T(8,128)(2,1)S(1)}, bf16[512,1792]{1,0:T(8,128)(2,1)}, u32[]{:S(2)}) copy-start(bf16[512,1792]{1,0:T(8,128)(2,1)} %param.7) | copy-start | bytes 5505028
  34.7 10.8 %copy-start.2 = (bf16[1792,512]{1,0:T(8,128)(2,1)S(1)}, bf16[1792,512]{1,0:T(8,128)(2,1)}, u32[]{:S(2)}) copy-start(bf16[1792,512]{1,0:T(8,128)(2,1)} %param.9) | copy-start | bytes 5505028
  35.2 12.4 %collective-permute-start = (f32[64,3584]{1,0:T(8,128)S(1)}, f32[64,3584]{1,0:T(8,128)S(1)}, u32[]{:S(2)}, u32[]{:S(2)}) collective-permute-start(f32[64,3584]{1,0:T(8,128)S(1)} %pad_maximum_fusion), channel_id=1, source_target_pairs={{0,64},{64,0},{1,65},{65,1},{2,66},{66,2},{3,67},{67,3},{4,68},{68... | collective-permute-start | bytes 2752520 | tf_op jit(solution)/shard_map/ppermute | solution.py:192
  46.6 13.2 %copy-start.1 = (f32[1792]{0:T(1024)S(1)}, f32[1792]{0:T(1024)}, u32[]{:S(2)}) copy-start(f32[1792]{0:T(1024)} %param.8) | copy-start | bytes 21508
  75.8 21.8 %all-to-all-start.2 = ((bf16[8,24,448]{2,1,0:T(8,128)(2,1)}), bf16[8,24,448]{2,1,0:T(8,128)(2,1)S(1)}, u32[]{:S(2)}, u32[]{:S(2)}) async-start(bf16[8,24,448]{2,1,0:T(8,128)(2,1)} %get-tuple-element.15), calls=%async_computation.2 | async-start | bytes 393216 | tf_op jit(solution)/shard_map/all_to_all | solution.py:196
  84.4 1.5 %copy-start.3 = (bf16[1792,512]{1,0:T(8,128)(2,1)S(1)}, bf16[1792,512]{1,0:T(8,128)(2,1)}, u32[]{:S(2)}) copy-start(bf16[1792,512]{1,0:T(8,128)(2,1)} %param.9) | copy-start | bytes 5505028
  97.6 43.3 %all-to-all-start.1 = ((bf16[8,16,1024]{2,1,0:T(8,128)(2,1)}), bf16[8,16,1024]{2,1,0:T(8,128)(2,1)S(1)}, u32[]{:S(2)}, u32[]{:S(2)}) async-start(bf16[8,16,1024]{2,1,0:T(8,128)(2,1)} %bitcast.9), calls=%async_computation.1 | async-start | bytes 524288 | tf_op jit(solution)/shard_map/all_to_all | solution.py:202
  106.7 25.3 %collective-permute-start.1 = (bf16[512,512]{1,0:T(8,128)(2,1)S(1)}, bf16[512,512]{1,0:T(8,128)(2,1)S(1)}, u32[]{:S(2)}, u32[]{:S(2)}) collective-permute-start(bf16[512,512]{1,0:T(8,128)(2,1)S(1)} %all_gather.12.x0_ref), channel_id=1, source_target_pairs={{0,1},{1,2},{2,3},{3,0},{4,5},{5,6},{6,7},{7,4},{8,9},{9,10},{10,1... | collective-permute-start | bytes 1572872 | tf_op jit(solution)/shard_map/ppermute | solution.py:181
  110.4 21.6 %collective-permute-start.2 = (bf16[512,512]{1,0:T(8,128)(2,1)S(1)}, bf16[512,512]{1,0:T(8,128)(2,1)S(1)}, u32[]{:S(2)}, u32[]{:S(2)}) collective-permute-start(bf16[512,512]{1,0:T(8,128)(2,1)S(1)} %all_gather.12.x0_ref), channel_id=1, source_target_pairs={{0,2},{1,3},{2,0},{3,1},{4,6},{5,7},{6,4},{7,5},{8,10},{9,11},{10,... | collective-permute-start | bytes 1572872 | tf_op jit(solution)/shard_map/ppermute | solution.py:181
  112.9 26.1 %collective-permute-start.3 = (bf16[512,512]{1,0:T(8,128)(2,1)S(1)}, bf16[512,512]{1,0:T(8,128)(2,1)S(1)}, u32[]{:S(2)}, u32[]{:S(2)}) collective-permute-start(bf16[512,512]{1,0:T(8,128)(2,1)S(1)} %all_gather.12.x0_ref), channel_id=1, source_target_pairs={{0,3},{1,0},{2,1},{3,2},{4,7},{5,4},{6,5},{7,6},{8,11},{9,8},{10,9... | collective-permute-start | bytes 1572872 | tf_op jit(solution)/shard_map/ppermute | solution.py:181

commit v5 on v4

--- a/solution.py
+++ b/solution.py
@@ -39,41 +39,50 @@
     return hi, (v - hi.astype(f32)).astype(bf16)
 
 
-def gelu_body(dep_n, recv_ref, bias_ref, hid_ref, send_ref):
-    y_n, tile, wide = recv_ref.shape
+def gelu_body(zh_n, x_n, recv_ref, bias_ref, hid_ref, send_ref, both_ref):
+    y_n, rows_n, wide = recv_ref.shape
     f_loc = wide // 2
-    part = f_loc // dep_n
-    half = dep_n // 2
+    tile = rows_n // zh_n
+    far = f_loc // zh_n
+    part = far // x_n
+    half = f_loc // (2 * part)
+    my_zh = lax.axis_index("zh")
     pre = recv_ref[0].astype(f32)
     for j in range(1, y_n):
         pre = pre + recv_ref[j].astype(f32)
     bias = jnp.concatenate([bias_ref[j : j + 1, :] for j in range(bias_ref.shape[0])], axis=1)
     value, slope = gelu_parts(pre[:, :f_loc] + bias)
     pre_grad = pre[:, f_loc:] * slope
-    hid_ref[:, :f_loc] = value.astype(bf16)
-    hid_ref[:, f_loc:] = pre_grad.astype(bf16)
+    both_ref[:, :f_loc] = value.astype(bf16)
+    both_ref[:, f_loc:] = pre_grad.astype(bf16)
+    hid_ref[...] = both_ref[pl.ds(pl.multiple_of(my_zh * tile, tile), tile), :]
     rows = jnp.sum(pre_grad, axis=0, keepdims=True)
     high = rows.astype(bf16).astype(f32)
     extra = [v[:, j * 2 * part : (j + 1) * 2 * part] for v in (high, rows - high) for j in range(half)]
     extra = jnp.concatenate(extra, axis=0).astype(bf16)
-    for d in range(dep_n):
-        cut = slice(d * part, (d + 1) * part)
-        send_ref[d, :tile] = jnp.concatenate([value[:, cut], pre_grad[:, cut]], axis=1).astype(bf16)
-        send_ref[d, tile:] = extra
-
-
-def gelu_stage(recv, bias, dep_n):
-    _, tile, wide = recv.shape
+    near = my_zh == 0
+    value = jnp.where(near, value[:, :far], value[:, far:])
+    pre_grad = jnp.where(near, pre_grad[:, :far], pre_grad[:, far:])
+    for x in range(x_n):
+        cut = slice(x * part, (x + 1) * part)
+        send_ref[x, :rows_n] = jnp.concatenate([value[:, cut], pre_grad[:, cut]], axis=1).astype(bf16)
+        send_ref[x, rows_n:] = extra
+
+
+def gelu_stage(recv, bias, zh_n, x_n):
+    _, rows_n, wide = recv.shape
+    dep_n = zh_n * x_n
     vmem = pl.BlockSpec(memory_space=pltpu.VMEM)
     return pl.pallas_call(
-        functools.partial(gelu_body, dep_n),
+        functools.partial(gelu_body, zh_n, x_n),
         in_specs=[vmem, vmem],
         out_specs=(vmem, vmem),
         out_shape=(
-            jax.ShapeDtypeStruct((tile, wide), bf16),
-            jax.ShapeDtypeStruct((dep_n, tile + dep_n, wide // dep_n), bf16),
+            jax.ShapeDtypeStruct((rows_n // zh_n, wide), bf16),
+            jax.ShapeDtypeStruct((x_n, rows_n + dep_n, wide // dep_n), bf16),
         ),
-        compiler_params=pltpu.CompilerParams(vmem_limit_bytes=8 << 20),
+        scratch_shapes=[pltpu.VMEM((rows_n, wide), bf16)],
+        compiler_params=pltpu.CompilerParams(vmem_limit_bytes=16 << 20),
         name="gelu_stage",
     )(in_vmem(recv), bias.reshape(-1, 128))
 
@@ -104,7 +113,7 @@
     for k, x_ref in enumerate(x_refs):
         src_x = lax.rem(my_x + (x_n - k), x_n)
         for zh in range(zh_n):
-            at = pl.multiple_of((zh * x_n + src_x) * tile, tile)
+            at = pl.multiple_of((src_x * zh_n + zh) * tile, tile)
             for j in range(col_n):
                 to = (zh * col_n + j) * tile
                 h_ref[k, to : to + tile, :] = hid_ref[j, pl.ds(at, tile), :]
@@ -179,21 +188,20 @@
     others = []
     for k in range(1, x_n):
         others.append(lax.ppermute(zall, "x", [(i, (i + k) % x_n) for i in range(x_n)]))
-    mine = lax.dynamic_index_in_dim(
-        zall.reshape(zh_n, y_n, 2, 2, tile, d_loc), lax.axis_index("zh"), 0, keepdims=False
-    )
-
-    def first_products(core):
-        blk = lax.dynamic_index_in_dim(mine, core, 1, keepdims=False)
-        part_in = dot_nn(blk[:, 0].reshape(y_n * tile, d_loc), w_in)
-        part_out = dot_nt(blk[:, 1].reshape(y_n * tile, d_loc), w_out)
+    mine = zall.reshape(zh_n, y_n, 2, 2, tile, d_loc)
+
+    def first_products(core, kind):
+        blk = lax.dynamic_index_in_dim(mine, core, 2, keepdims=False).transpose(2, 1, 0, 3, 4)
+        blk = blk.reshape(2, y_n * zh_n * tile, d_loc)
+        part_in = dot_nn(blk[0], w_in).astype(kind)
+        part_out = dot_nt(blk[1], w_out).astype(kind)
         return jnp.concatenate([part_in, part_out], axis=1)
 
-    from_core = lax.ppermute(first_products(1 - my_core), "core", swap)
-    pre = (first_products(my_core) + from_core).astype(bf16)
-    pre = lax.all_to_all(pre.reshape(y_n, tile, 2 * f_loc), "y", 0, 0)
-    hid, send = gelu_stage(pre, b_in, dep_n)
-    got = lax.all_to_all(send, ("zh", "x"), 0, 0)
+    from_core = lax.ppermute(first_products(1 - my_core, bf16), "core", swap)
+    pre = (first_products(my_core, f32) + from_core.astype(f32)).astype(bf16)
+    pre = lax.all_to_all(pre.reshape(y_n, zh_n * tile, 2 * f_loc), "y", 0, 0)
+    hid, send = gelu_stage(pre, b_in, zh_n, x_n)
+    got = lax.all_to_all(send, "x", 0, 0)
     rows = lax.all_gather(hid, ("y", "core"), axis=0, tiled=True)
     outs = jnp.concatenate(
         [dot_nn(rows[:, :f_loc], w_out).astype(bf16), dot_nt(rows[:, f_loc:], w_in).astype(bf16)],
@@ -202,9 +210,10 @@
     outs = lax.all_to_all(outs.reshape(2 * y_n, tile, 2 * d_loc), ("zq", "zp"), 0, 0)
     block_out, tokens_grad = final_stage(outs)
 
-    b_sum = jnp.sum(got[:, tile : tile + half].astype(f32) + got[:, tile + half :].astype(f32), axis=0)
+    tall = zh_n * tile
+    b_sum = jnp.sum(got[:, tall : tall + half].astype(f32) + got[:, tall + half :].astype(f32), axis=0)
     b_pair = jnp.concatenate(hi_lo(b_sum), axis=0)
-    wsend = jnp.concatenate([got[:, :tile].reshape(dep_n * tile, 2 * part), b_pair], axis=0)
+    wsend = jnp.concatenate([got[:, :tall].reshape(dep_n * tile, 2 * part), b_pair], axis=0)
     wall = lax.all_gather(wsend, ("y", "core"), axis=0, tiled=False)
     w_in_grad, w_out_grad, b_in_grad = weight_stage([zall] + others, wall, dep_n)
     return (block_out, tokens_grad, w_in_grad.T, w_out_grad, b_in_grad.reshape(f_loc))

time: 142 us -> 129 us (0.908)
  starting transfers between devices: 36.2 us -> 27.5 us
  waiting for transfers between devices: 18.4 us -> 10.6 us
  blocking collectives: 75.1 us -> 79.4 us
  matrix products: 4.85 us -> 3.38 us
    all_to_all x1, waiting for transfers between devices: 10.5 us -> 2.49 us  [step(): got = lax.all_to_all(send, 'x', 0, 0)]
    all_to_all x1, blocking collectives: 12.2 us -> 16.8 us  [step(): pre = lax.all_to_all(pre.reshape(y_n, zh_n * tile, 2 * f_loc), 'y', 0, 0)]
    all_to_all x1, starting transfers between devices: 9.1 us -> 4.66 us  [step(): lax.all_to_all(outs.reshape(2 * y_n, tile, 2 * d_loc), ('zq', 'zp'), 0, 0)]
    all_to_all x1, starting transfers between devices: 8.65 us -> 4.22 us  [step(): got = lax.all_to_all(send, 'x', 0, 0)]
  transfers between devices with their start and end apart: 6 -> 6, of which waited for: 3 -> 3; matrix products, arithmetic and copies ran while one was open for 2% -> 2% of each run, Pallas kernels for 1% -> 2%
where the time goes in v5:
time: 129 us
  blocking collectives  79.4 us (62%)
  starting transfers between devices  27.5 us (21%)
  waiting for transfers between devices  10.6 us (8%)
  Pallas kernels  3.64 us (3%)
  matrix products  3.38 us (3%)
  other arithmetic  1.86 us (1%)
  local copies, waits for them, and re-layouts  1.53 us (1%)
    all_gather x1, blocking collectives, step(): zall = lax.all_gather(both, ('zh', 'zq', 'zp'), axis=0, tiled=True)  31 us
    all_to_all x1, blocking collectives, step(): pre = lax.all_to_all(pre.reshape(y_n, zh_n * tile, 2 * f_loc), 'y', 0, 0)  16.8 us
    all_gather x1, blocking collectives, step(): wall = lax.all_gather(wsend, ('y', 'core'), axis=0, tiled=False)  16.4 us
    all_gather x1, blocking collectives, step(): rows = lax.all_gather(hid, ('y', 'core'), axis=0, tiled=True)  15.2 us
    ppermute x1, starting transfers between devices, step(): from_core = lax.ppermute(first_products(1 - my_core, bf16), 'core', swap)  10.1 us
    ppermute x3, starting transfers between devices, step(): lax.ppermute(zall, 'x', [(i, (i + k) % x_n) for i in range(x_n)])  8.46 us
    ppermute x3, waiting for transfers between devices, step(): lax.ppermute(zall, 'x', [(i, (i + k) % x_n) for i in range(x_n)])  7.22 us
    all_to_all x1, starting transfers between devices, step(): lax.all_to_all(outs.reshape(2 * y_n, tile, 2 * d_loc), ('zq', 'zp'), 0, 0)  4.66 us
  transfers between devices with their start and end apart: 6, of which 3 were waited for; matrix products, arithmetic and copies ran while one was open for 2% of the time, Pallas kernels for 2%

profile of v5, /device:TPU:7, one launch (start us, length us, event | category | flops | bytes accessed | tf_op | source)
XLA Modules:
  0.0 128.8 jit_solution(8764273870277587573)
XLA Ops:
  0.6 0.0 copy-start
  0.7 0.9 pad_maximum_fusion.3
  1.5 31.0 %all_gather.12.x0_ref = bf16[512,512]{1,0:T(8,128)(2,1)S(1)} all-gather(bf16[32,512]{1,0:T(8,128)(2,1)S(1)} %pad_maximum_fusion.3), channel_id=1, replica_groups=mesh['y'=4,'core'=2,'zq'=4,'zp'=2,'zh'=2,'x'=4] {'zh','zq','zp'}, dimensions={0}, use_global_device_ids=true | all-gather | bytes 557056 | tf_op jit(solution)/shard_map/all_gather | solution.py:187
  32.5 0.0 copy-start.2
  32.6 1.4 %copy-done.2 = bf16[1792,512]{1,0:T(8,128)(2,1)S(1)} copy-done((bf16[1792,512]{1,0:T(8,128)(2,1)S(1)}, bf16[1792,512]{1,0:T(8,128)(2,1)}, u32[]{:S(2)}) %copy-start.2) | copy-done | bytes 1835032
  34.0 0.7 convolution_convert_fusion
  34.7 0.0 copy-done
  34.7 0.4 convolution_convert_fusion.1
  35.1 0.1 pad_maximum_fusion
  35.2 10.1 %collective-permute-start = (bf16[128,3584]{1,0:T(8,128)(2,1)S(1)}, bf16[128,3584]{1,0:T(8,128)(2,1)S(1)}, u32[]{:S(2)}, u32[]{:S(2)}) collective-permute-start(bf16[128,3584]{1,0:T(8,128)(2,1)S(1)} %pad_maximum_fusion), channel_id=1, source_target_pairs={{0,64},{64,0},{1,65},{65,1},{2,66},{66,2},{3,67},{67,3},{4,68},{68... | collective-permute-start | bytes 2752520 | tf_op jit(solution)/shard_map/ppermute | solution.py:200
  45.4 0.4 fusion.5
  45.8 0.7 fusion.6
  46.5 0.9 collective-permute-done
  47.4 0.2 fusion
  47.6 0.0 copy-start.1
  47.6 16.8 %all_to_all.15.recv_ref = bf16[4,32,3584]{2,1,0:T(8,128)(2,1)S(1)} all-to-all(bf16[4,32,3584]{2,1,0:T(8,128)(2,1)S(1)} %bitcast.33), channel_id=1, replica_groups=mesh['y'=4,'core'=2,'zq'=4,'zp'=2,'zh'=2,'x'=4] {'y'}, dimensions={0} | all-to-all | bytes 1835008 | tf_op jit(solution)/shard_map/all_to_all | solution.py:202
  64.4 0.0 copy-done.1
  64.4 1.1 gelu_stage.1
  65.5 15.2 %all_gather.13 = bf16[128,3584]{1,0:T(8,128)(2,1)S(1)} all-gather(bf16[16,3584]{1,0:T(8,128)(2,1)S(1)} %get-tuple-element.12), channel_id=1, replica_groups=mesh['y'=4,'core'=2,'zq'=4,'zp'=2,'zh'=2,'x'=4] {'y','core'}, dimensions={0}, use_global_device_ids=true | all-gather | bytes 1032192 | tf_op jit(solution)/shard_map/all_gather | solution.py:205
  80.7 0.7 convolution_convert_fusion.2
  81.5 0.4 convolution_convert_fusion.3
  81.9 4.2 %all-to-all-start.2 = ((bf16[4,40,448]{2,1,0:T(8,128)(2,1)}), bf16[4,40,448]{2,1,0:T(8,128)(2,1)S(1)}, u32[]{:S(2)}, u32[]{:S(2)}) async-start(bf16[4,40,448]{2,1,0:T(8,128)(2,1)} %get-tuple-element.15), calls=%async_computation.2 | async-start | bytes 327680 | tf_op jit(solution)/shard_map/all_to_all | solution.py:204
  86.1 0.7 pad_maximum_fusion.1
  86.8 2.5 %all-to-all-done.2 = bf16[4,40,448]{2,1,0:T(8,128)(2,1)S(1)} async-done(((bf16[4,40,448]{2,1,0:T(8,128)(2,1)}), bf16[4,40,448]{2,1,0:T(8,128)(2,1)S(1)}, u32[]{:S(2)}, u32[]{:S(2)}) %all-to-all-start.2) | async-done | bytes 143392 | tf_op jit(solution)/shard_map/all_to_all | solution.py:204
  89.3 4.7 %all-to-all-start.1 = ((bf16[8,16,1024]{2,1,0:T(8,128)(2,1)}), bf16[8,16,1024]{2,1,0:T(8,128)(2,1)S(1)}, u32[]{:S(2)}, u32[]{:S(2)}) async-start(bf16[8,16,1024]{2,1,0:T(8,128)(2,1)} %bitcast.13), calls=%async_computation.1 | async-start | bytes 524288 | tf_op jit(solution)/shard_map/all_to_all | solution.py:210
  94.0 3.7 %collective-permute-start.1 = (bf16[512,512]{1,0:T(8,128)(2,1)S(1)}, bf16[512,512]{1,0:T(8,128)(2,1)S(1)}, u32[]{:S(2)}, u32[]{:S(2)}) collective-permute-start(bf16[512,512]{1,0:T(8,128)(2,1)S(1)} %all_gather.12.x0_ref), channel_id=1, source_target_pairs={{0,1},{1,2},{2,3},{3,0},{4,5},{5,6},{6,7},{7,4},{8,9},{9,10},{10,1... | collective-permute-start | bytes 1572872 | tf_op jit(solution)/shard_map/ppermute | solution.py:190
  97.7 2.0 %collective-permute-start.2 = (bf16[512,512]{1,0:T(8,128)(2,1)S(1)}, bf16[512,512]{1,0:T(8,128)(2,1)S(1)}, u32[]{:S(2)}, u32[]{:S(2)}) collective-permute-start(bf16[512,512]{1,0:T(8,128)(2,1)S(1)} %all_gather.12.x0_ref), channel_id=1, source_target_pairs={{0,2},{1,3},{2,0},{3,1},{4,6},{5,7},{6,4},{7,5},{8,10},{9,11},{10,... | collective-permute-start | bytes 1572872 | tf_op jit(solution)/shard_map/ppermute | solution.py:190
  99.7 2.7 %collective-permute-start.3 = (bf16[512,512]{1,0:T(8,128)(2,1)S(1)}, bf16[512,512]{1,0:T(8,128)(2,1)S(1)}, u32[]{:S(2)}, u32[]{:S(2)}) collective-permute-start(bf16[512,512]{1,0:T(8,128)(2,1)S(1)} %all_gather.12.x0_ref), channel_id=1, source_target_pairs={{0,3},{1,0},{2,1},{3,2},{4,7},{5,4},{6,5},{7,6},{8,11},{9,8},{10,9... | collective-permute-start | bytes 1572872 | tf_op jit(solution)/shard_map/ppermute | solution.py:190
  102.5 16.4 %all-gather = bf16[1088,448]{1,0:T(8,128)(2,1)S(1)} all-gather(bf16[136,448]{1,0:T(8,128)(2,1)S(1)} %pad_maximum_fusion.2), channel_id=2, replica_groups=mesh['y'=4,'core'=2,'zq'=4,'zp'=2,'zh'=2,'x'=4] {'y','core'}, dimensions={0}, use_global_device_ids=true | all-gather | bytes 1096704 | tf_op jit(solution)/shard_map/all_gather | solution.py:217
  118.9 0.0 collective-permute-done.1.x1_ref
  118.9 0.0 collective-permute-done.2.x2_ref
  118.9 7.2 %collective-permute-done.3.x3_ref = bf16[512,512]{1,0:T(8,128)(2,1)S(1)} collective-permute-done((bf16[512,512]{1,0:T(8,128)(2,1)S(1)}, bf16[512,512]{1,0:T(8,128)(2,1)S(1)}, u32[]{:S(2)}, u32[]{:S(2)}) %collective-permute-start.3) | collective-permute-done | bytes 524320 | tf_op jit(solution)/shard_map/ppermute | solution.py:190
  126.2 1.9 %weight_stage.1 = (bf16[224,512]{1,0:T(8,128)(2,1)}, bf16[224,512]{1,0:T(8,128)(2,1)}, f32[14,128]{1,0:T(8,128)}) custom-call(bf16[512,512]{1,0:T(8,128)(2,1)S(1)} %all_gather.12.x0_ref, bf16[512,512]{1,0:T(8,128)(2,1)S(1)} %collective-permute-done.1.x1_ref, bf16[512,512]{1,0:T(8,128)(2,1)S(1)} %collective-permute-done.2.x2_ref, ...), custom_call_target="tpu_custom_call" | custom-call | tf_op jit(solution)/shard_map/weight_stage/pallas_call | solution.py:156
  128.1 0.0 all-to-all-done.1.parts_ref
  128.1 0.6 final_stage.1
  (8 shorter events, 0.2 us)
Async XLA Ops:
  0.6 34.1 %copy-start = (bf16[512,1792]{1,0:T(8,128)(2,1)S(1)}, bf16[512,1792]{1,0:T(8,128)(2,1)}, u32[]{:S(2)}) copy-start(bf16[512,1792]{1,0:T(8,128)(2,1)} %param.7) | copy-start | bytes 5505028
  32.5 1.5 %copy-start.2 = (bf16[1792,512]{1,0:T(8,128)(2,1)S(1)}, bf16[1792,512]{1,0:T(8,128)(2,1)}, u32[]{:S(2)}) copy-start(bf16[1792,512]{1,0:T(8,128)(2,1)} %param.9) | copy-start | bytes 5505028
  35.2 12.2 %collective-permute-start = (bf16[128,3584]{1,0:T(8,128)(2,1)S(1)}, bf16[128,3584]{1,0:T(8,128)(2,1)S(1)}, u32[]{:S(2)}, u32[]{:S(2)}) collective-permute-start(bf16[128,3584]{1,0:T(8,128)(2,1)S(1)} %pad_maximum_fusion), channel_id=1, source_target_pairs={{0,64},{64,0},{1,65},{65,1},{2,66},{66,2},{3,67},{67,3},{4,68},{68... | collective-permute-start | bytes 2752520 | tf_op jit(solution)/shard_map/ppermute | solution.py:200
  47.6 16.8 %copy-start.1 = (f32[1792]{0:T(1024)S(1)}, f32[1792]{0:T(1024)}, u32[]{:S(2)}) copy-start(f32[1792]{0:T(1024)} %param.8) | copy-start | bytes 21508
  81.9 7.4 %all-to-all-start.2 = ((bf16[4,40,448]{2,1,0:T(8,128)(2,1)}), bf16[4,40,448]{2,1,0:T(8,128)(2,1)S(1)}, u32[]{:S(2)}, u32[]{:S(2)}) async-start(bf16[4,40,448]{2,1,0:T(8,128)(2,1)} %get-tuple-element.15), calls=%async_computation.2 | async-start | bytes 327680 | tf_op jit(solution)/shard_map/all_to_all | solution.py:204
  89.3 38.8 %all-to-all-start.1 = ((bf16[8,16,1024]{2,1,0:T(8,128)(2,1)}), bf16[8,16,1024]{2,1,0:T(8,128)(2,1)S(1)}, u32[]{:S(2)}, u32[]{:S(2)}) async-start(bf16[8,16,1024]{2,1,0:T(8,128)(2,1)} %bitcast.13), calls=%async_computation.1 | async-start | bytes 524288 | tf_op jit(solution)/shard_map/all_to_all | solution.py:210
  94.0 25.0 %collective-permute-start.1 = (bf16[512,512]{1,0:T(8,128)(2,1)S(1)}, bf16[512,512]{1,0:T(8,128)(2,1)S(1)}, u32[]{:S(2)}, u32[]{:S(2)}) collective-permute-start(bf16[512,512]{1,0:T(8,128)(2,1)S(1)} %all_gather.12.x0_ref), channel_id=1, source_target_pairs={{0,1},{1,2},{2,3},{3,0},{4,5},{5,6},{6,7},{7,4},{8,9},{9,10},{10,1... | collective-permute-start | bytes 1572872 | tf_op jit(solution)/shard_map/ppermute | solution.py:190
  97.7 21.3 %collective-permute-start.2 = (bf16[512,512]{1,0:T(8,128)(2,1)S(1)}, bf16[512,512]{1,0:T(8,128)(2,1)S(1)}, u32[]{:S(2)}, u32[]{:S(2)}) collective-permute-start(bf16[512,512]{1,0:T(8,128)(2,1)S(1)} %all_gather.12.x0_ref), channel_id=1, source_target_pairs={{0,2},{1,3},{2,0},{3,1},{4,6},{5,7},{6,4},{7,5},{8,10},{9,11},{10,... | collective-permute-start | bytes 1572872 | tf_op jit(solution)/shard_map/ppermute | solution.py:190
  99.7 26.4 %collective-permute-start.3 = (bf16[512,512]{1,0:T(8,128)(2,1)S(1)}, bf16[512,512]{1,0:T(8,128)(2,1)S(1)}, u32[]{:S(2)}, u32[]{:S(2)}) collective-permute-start(bf16[512,512]{1,0:T(8,128)(2,1)S(1)} %all_gather.12.x0_ref), channel_id=1, source_target_pairs={{0,3},{1,0},{2,1},{3,2},{4,7},{5,4},{6,5},{7,6},{8,11},{9,8},{10,9... | collective-permute-start | bytes 1572872 | tf_op jit(solution)/shard_map/ppermute | solution.py:190

commit v6 on v5

--- a/solution.py
+++ b/solution.py
@@ -131,6 +131,31 @@
     return pltpu.with_memory_space_constraint(x, pltpu.VMEM)
 
 
+def product_body(rows_ref, win_ref, wout_ref, out_ref, win_buf, sem):
+    load = pltpu.make_async_copy(win_ref, win_buf, sem.at[0])
+    load.start()
+    n, tile, wide = out_ref.shape
+    f_loc = rows_ref.shape[1] // 2
+    first = dot_nn(rows_ref[:, :f_loc], wout_ref[...]).astype(bf16)
+    out_ref[:, :, : wide // 2] = first.reshape(n, tile, wide // 2)
+    load.wait()
+    second = dot_nt(rows_ref[:, f_loc:], win_buf[...]).astype(bf16)
+    out_ref[:, :, wide // 2 :] = second.reshape(n, tile, wide // 2)
+
+
+def product_stage(rows, w_in, w_out, tile):
+    vmem = pl.BlockSpec(memory_space=pltpu.VMEM)
+    return pl.pallas_call(
+        product_body,
+        in_specs=[vmem, pl.BlockSpec(memory_space=pl.ANY), vmem],
+        out_specs=vmem,
+        out_shape=jax.ShapeDtypeStruct((rows.shape[0] // tile, tile, 2 * w_in.shape[0]), bf16),
+        scratch_shapes=[pltpu.VMEM(w_in.shape, bf16), pltpu.SemaphoreType.DMA((1,))],
+        compiler_params=pltpu.CompilerParams(vmem_limit_bytes=16 << 20),
+        name="product_stage",
+    )(in_vmem(rows), w_in, in_vmem(w_out))
+
+
 def final_body(parts_ref, first_ref, second_ref):
     n, _, wide = parts_ref.shape
     total = parts_ref[0].astype(f32)
@@ -203,11 +228,8 @@
     hid, send = gelu_stage(pre, b_in, zh_n, x_n)
     got = lax.all_to_all(send, "x", 0, 0)
     rows = lax.all_gather(hid, ("y", "core"), axis=0, tiled=True)
-    outs = jnp.concatenate(
-        [dot_nn(rows[:, :f_loc], w_out).astype(bf16), dot_nt(rows[:, f_loc:], w_in).astype(bf16)],
-        axis=1,
-    )
-    outs = lax.all_to_all(outs.reshape(2 * y_n, tile, 2 * d_loc), ("zq", "zp"), 0, 0)
+    outs = product_stage(rows, w_in, w_out, tile)
+    outs = lax.all_to_all(outs, ("zq", "zp"), 0, 0)
     block_out, tokens_grad = final_stage(outs)
 
     tall = zh_n * tile

time: 129 us -> 128 us (level)
  the two profiles are of different devices: /device:TPU:7 before, /device:TPU:3 now
where the time goes in v6:
time: 128 us; the launch traced here: 127 us
  blocking collectives  78.7 us (61%)
  starting transfers between devices  28.6 us (22%)
  waiting for transfers between devices  7.71 us (6%)
  Pallas kernels  5.59 us (4%)
  local copies, waits for them, and re-layouts  2.32 us (2%)
  matrix products  2.26 us (2%)
    all_gather x1, blocking collectives, step(): zall = lax.all_gather(both, ('zh', 'zq', 'zp'), axis=0, tiled=True)  31 us
    all_to_all x1, blocking collectives, step(): pre = lax.all_to_all(pre.reshape(y_n, zh_n * tile, 2 * f_loc), 'y', 0, 0)  16.8 us
    all_gather x1, blocking collectives, step(): rows = lax.all_gather(hid, ('y', 'core'), axis=0, tiled=True)  15.8 us
    all_gather x1, blocking collectives, step(): wall = lax.all_gather(wsend, ('y', 'core'), axis=0, tiled=False)  15.1 us
    ppermute x1, starting transfers between devices, step(): from_core = lax.ppermute(first_products(1 - my_core, bf16), 'core', swap)  10.1 us
    ppermute x3, starting transfers between devices, step(): lax.ppermute(zall, 'x', [(i, (i + k) % x_n) for i in range(x_n)])  9.57 us
    ppermute x3, waiting for transfers between devices, step(): lax.ppermute(zall, 'x', [(i, (i + k) % x_n) for i in range(x_n)])  6.8 us
    all_to_all x1, starting transfers between devices, step(): outs = lax.all_to_all(outs, ('zq', 'zp'), 0, 0)  4.67 us
  transfers between devices with their start and end apart: 6, of which 2 were waited for; matrix products, arithmetic and copies ran while one was open for 1% of the time, Pallas kernels for 3%

profile of v6, /device:TPU:3, one launch (start us, length us, event | category | flops | bytes accessed | tf_op | source)
XLA Modules:
  0.0 127.2 jit_solution(12133717908535995220)
XLA Ops:
  0.6 0.0 copy-start
  0.6 0.9 pad_maximum_fusion.2
  1.5 31.0 %all_gather.12.x0_ref = bf16[512,512]{1,0:T(8,128)(2,1)S(1)} all-gather(bf16[32,512]{1,0:T(8,128)(2,1)S(1)} %pad_maximum_fusion.2), channel_id=1, replica_groups=mesh['y'=4,'core'=2,'zq'=4,'zp'=2,'zh'=2,'x'=4] {'zh','zq','zp'}, dimensions={0}, use_global_device_ids=true | all-gather | bytes 557056 | tf_op jit(solution)/shard_map/all_gather | solution.py:212
  32.5 0.0 copy-start.1
  32.6 0.0 copy-done
  32.6 0.7 convolution_convert_fusion
  33.3 0.7 copy-done.1
  34.0 0.4 convolution_convert_fusion.1
  34.4 0.1 pad_maximum_fusion
  34.5 10.1 %collective-permute-start = (bf16[128,3584]{1,0:T(8,128)(2,1)S(1)}, bf16[128,3584]{1,0:T(8,128)(2,1)S(1)}, u32[]{:S(2)}, u32[]{:S(2)}) collective-permute-start(bf16[128,3584]{1,0:T(8,128)(2,1)S(1)} %pad_maximum_fusion), channel_id=1, source_target_pairs={{0,64},{64,0},{1,65},{65,1},{2,66},{66,2},{3,67},{67,3},{4,68},{68... | collective-permute-start | bytes 2752520 | tf_op jit(solution)/shard_map/ppermute | solution.py:225
  44.7 0.4 fusion.3
  45.1 0.7 fusion.4
  45.8 0.9 collective-permute-done
  46.7 0.2 fusion
  46.9 0.0 copy-start.3
  46.9 16.8 %all_to_all.15.recv_ref = bf16[4,32,3584]{2,1,0:T(8,128)(2,1)S(1)} all-to-all(bf16[4,32,3584]{2,1,0:T(8,128)(2,1)S(1)} %bitcast.30), channel_id=1, replica_groups=mesh['y'=4,'core'=2,'zq'=4,'zp'=2,'zh'=2,'x'=4] {'y'}, dimensions={0} | all-to-all | bytes 1835008 | tf_op jit(solution)/shard_map/all_to_all | solution.py:227
  63.7 0.0 copy-done.3
  63.7 1.1 gelu_stage.1
  64.8 4.3 %all-to-all-start.2 = ((bf16[4,40,448]{2,1,0:T(8,128)(2,1)}), bf16[4,40,448]{2,1,0:T(8,128)(2,1)S(1)}, u32[]{:S(2)}, u32[]{:S(2)}) async-start(bf16[4,40,448]{2,1,0:T(8,128)(2,1)} %get-tuple-element.15), calls=%async_computation.2 | async-start | bytes 327680 | tf_op jit(solution)/shard_map/all_to_all | solution.py:229
  69.1 15.8 %all_gather.13.rows_ref = bf16[128,3584]{1,0:T(8,128)(2,1)S(1)} all-gather(bf16[16,3584]{1,0:T(8,128)(2,1)S(1)} %get-tuple-element.12), channel_id=1, replica_groups=mesh['y'=4,'core'=2,'zq'=4,'zp'=2,'zh'=2,'x'=4] {'y','core'}, dimensions={0}, use_global_device_ids=true | all-gather | bytes 1032192 | tf_op jit(solution)/shard_map/all_gather | solution.py:230
  84.9 0.0 copy-start.2
  84.9 1.5 %copy-done.2 = bf16[512,1792]{1,0:T(8,128)(2,1)S(1)} copy-done((bf16[512,1792]{1,0:T(8,128)(2,1)S(1)}, bf16[512,1792]{1,0:T(8,128)(2,1)}, u32[]{:S(2)}) %copy-start.2) | copy-done | bytes 1835032
  86.4 1.9 %product_stage.1 = bf16[8,16,1024]{2,1,0:T(8,128)(2,1)} custom-call(bf16[128,3584]{1,0:T(8,128)(2,1)S(1)} %all_gather.13.rows_ref, bf16[512,1792]{1,0:T(8,128)(2,1)S(1)} %copy-done.2, bf16[1792,512]{1,0:T(8,128)(2,1)S(1)} %copy-done), custom_call_target="tpu_custom_call" | custom-call | tf_op jit(solution)/shard_map/product_stage/pallas_call | solution.py:148
  88.3 0.0 all-to-all-done.2
  88.3 4.7 %all-to-all-start.1 = ((bf16[8,16,1024]{2,1,0:T(8,128)(2,1)}), bf16[8,16,1024]{2,1,0:T(8,128)(2,1)S(1)}, u32[]{:S(2)}, u32[]{:S(2)}) async-start(bf16[8,16,1024]{2,1,0:T(8,128)(2,1)} %product_stage.1), calls=%async_computation.1 | async-start | bytes 524288 | tf_op jit(solution)/shard_map/all_to_all | solution.py:232
  93.0 3.1 %collective-permute-start.1 = (bf16[512,512]{1,0:T(8,128)(2,1)S(1)}, bf16[512,512]{1,0:T(8,128)(2,1)S(1)}, u32[]{:S(2)}, u32[]{:S(2)}) collective-permute-start(bf16[512,512]{1,0:T(8,128)(2,1)S(1)} %all_gather.12.x0_ref), channel_id=1, source_target_pairs={{0,1},{1,2},{2,3},{3,0},{4,5},{5,6},{6,7},{7,4},{8,9},{9,10},{10,1... | collective-permute-start | bytes 1572872 | tf_op jit(solution)/shard_map/ppermute | solution.py:215
  96.1 2.5 %collective-permute-start.2 = (bf16[512,512]{1,0:T(8,128)(2,1)S(1)}, bf16[512,512]{1,0:T(8,128)(2,1)S(1)}, u32[]{:S(2)}, u32[]{:S(2)}) collective-permute-start(bf16[512,512]{1,0:T(8,128)(2,1)S(1)} %all_gather.12.x0_ref), channel_id=1, source_target_pairs={{0,2},{1,3},{2,0},{3,1},{4,6},{5,7},{6,4},{7,5},{8,10},{9,11},{10,... | collective-permute-start | bytes 1572872 | tf_op jit(solution)/shard_map/ppermute | solution.py:215
  98.6 4.0 %collective-permute-start.3 = (bf16[512,512]{1,0:T(8,128)(2,1)S(1)}, bf16[512,512]{1,0:T(8,128)(2,1)S(1)}, u32[]{:S(2)}, u32[]{:S(2)}) collective-permute-start(bf16[512,512]{1,0:T(8,128)(2,1)S(1)} %all_gather.12.x0_ref), channel_id=1, source_target_pairs={{0,3},{1,0},{2,1},{3,2},{4,7},{5,4},{6,5},{7,6},{8,11},{9,8},{10,9... | collective-permute-start | bytes 1572872 | tf_op jit(solution)/shard_map/ppermute | solution.py:215
  102.7 15.1 %all-gather = bf16[1088,448]{1,0:T(8,128)(2,1)S(1)} all-gather(bf16[136,448]{1,0:T(8,128)(2,1)S(1)} %pad_maximum_fusion.1), channel_id=2, replica_groups=mesh['y'=4,'core'=2,'zq'=4,'zp'=2,'zh'=2,'x'=4] {'y','core'}, dimensions={0}, use_global_device_ids=true | all-gather | bytes 1096704 | tf_op jit(solution)/shard_map/all_gather | solution.py:239
  117.8 0.0 collective-permute-done.1.x1_ref
  117.8 0.0 collective-permute-done.2.x2_ref
  117.8 6.8 %collective-permute-done.3.x3_ref = bf16[512,512]{1,0:T(8,128)(2,1)S(1)} collective-permute-done((bf16[512,512]{1,0:T(8,128)(2,1)S(1)}, bf16[512,512]{1,0:T(8,128)(2,1)S(1)}, u32[]{:S(2)}, u32[]{:S(2)}) %collective-permute-start.3) | collective-permute-done | bytes 524320 | tf_op jit(solution)/shard_map/ppermute | solution.py:215
  124.6 1.9 %weight_stage.1 = (bf16[224,512]{1,0:T(8,128)(2,1)}, bf16[224,512]{1,0:T(8,128)(2,1)}, f32[14,128]{1,0:T(8,128)}) custom-call(bf16[512,512]{1,0:T(8,128)(2,1)S(1)} %all_gather.12.x0_ref, bf16[512,512]{1,0:T(8,128)(2,1)S(1)} %collective-permute-done.1.x1_ref, bf16[512,512]{1,0:T(8,128)(2,1)S(1)} %collective-permute-done.2.x2_ref, ...), custom_call_target="tpu_custom_call" | custom-call | tf_op jit(solution)/shard_map/weight_stage/pallas_call | solution.py:181
  126.5 0.0 all-to-all-done.1.parts_ref
  126.5 0.6 final_stage.1
  (8 shorter events, 0.2 us)
Async XLA Ops:
  0.6 32.0 %copy-start = (bf16[1792,512]{1,0:T(8,128)(2,1)S(1)}, bf16[1792,512]{1,0:T(8,128)(2,1)}, u32[]{:S(2)}) copy-start(bf16[1792,512]{1,0:T(8,128)(2,1)} %wout_ref.1) | copy-start | bytes 5505028
  32.5 1.5 %copy-start.1 = (bf16[512,1792]{1,0:T(8,128)(2,1)S(1)}, bf16[512,1792]{1,0:T(8,128)(2,1)}, u32[]{:S(2)}) copy-start(bf16[512,1792]{1,0:T(8,128)(2,1)} %win_ref.1) | copy-start | bytes 5505028
  34.5 12.2 %collective-permute-start = (bf16[128,3584]{1,0:T(8,128)(2,1)S(1)}, bf16[128,3584]{1,0:T(8,128)(2,1)S(1)}, u32[]{:S(2)}, u32[]{:S(2)}) collective-permute-start(bf16[128,3584]{1,0:T(8,128)(2,1)S(1)} %pad_maximum_fusion), channel_id=1, source_target_pairs={{0,64},{64,0},{1,65},{65,1},{2,66},{66,2},{3,67},{67,3},{4,68},{68... | collective-permute-start | bytes 2752520 | tf_op jit(solution)/shard_map/ppermute | solution.py:225
  46.9 16.8 %copy-start.3 = (f32[1792]{0:T(1024)S(1)}, f32[1792]{0:T(1024)}, u32[]{:S(2)}) copy-start(f32[1792]{0:T(1024)} %param.8) | copy-start | bytes 21508
  64.8 23.5 %all-to-all-start.2 = ((bf16[4,40,448]{2,1,0:T(8,128)(2,1)}), bf16[4,40,448]{2,1,0:T(8,128)(2,1)S(1)}, u32[]{:S(2)}, u32[]{:S(2)}) async-start(bf16[4,40,448]{2,1,0:T(8,128)(2,1)} %get-tuple-element.15), calls=%async_computation.2 | async-start | bytes 327680 | tf_op jit(solution)/shard_map/all_to_all | solution.py:229
  84.9 1.5 %copy-start.2 = (bf16[512,1792]{1,0:T(8,128)(2,1)S(1)}, bf16[512,1792]{1,0:T(8,128)(2,1)}, u32[]{:S(2)}) copy-start(bf16[512,1792]{1,0:T(8,128)(2,1)} %win_ref.1) | copy-start | bytes 5505028
  88.3 38.2 %all-to-all-start.1 = ((bf16[8,16,1024]{2,1,0:T(8,128)(2,1)}), bf16[8,16,1024]{2,1,0:T(8,128)(2,1)S(1)}, u32[]{:S(2)}, u32[]{:S(2)}) async-start(bf16[8,16,1024]{2,1,0:T(8,128)(2,1)} %product_stage.1), calls=%async_computation.1 | async-start | bytes 524288 | tf_op jit(solution)/shard_map/all_to_all | solution.py:232
  93.0 24.8 %collective-permute-start.1 = (bf16[512,512]{1,0:T(8,128)(2,1)S(1)}, bf16[512,512]{1,0:T(8,128)(2,1)S(1)}, u32[]{:S(2)}, u32[]{:S(2)}) collective-permute-start(bf16[512,512]{1,0:T(8,128)(2,1)S(1)} %all_gather.12.x0_ref), channel_id=1, source_target_pairs={{0,1},{1,2},{2,3},{3,0},{4,5},{5,6},{6,7},{7,4},{8,9},{9,10},{10,1... | collective-permute-start | bytes 1572872 | tf_op jit(solution)/shard_map/ppermute | solution.py:215
  96.1 21.7 %collective-permute-start.2 = (bf16[512,512]{1,0:T(8,128)(2,1)S(1)}, bf16[512,512]{1,0:T(8,128)(2,1)S(1)}, u32[]{:S(2)}, u32[]{:S(2)}) collective-permute-start(bf16[512,512]{1,0:T(8,128)(2,1)S(1)} %all_gather.12.x0_ref), channel_id=1, source_target_pairs={{0,2},{1,3},{2,0},{3,1},{4,6},{5,7},{6,4},{7,5},{8,10},{9,11},{10,... | collective-permute-start | bytes 1572872 | tf_op jit(solution)/shard_map/ppermute | solution.py:215
  98.6 25.9 %collective-permute-start.3 = (bf16[512,512]{1,0:T(8,128)(2,1)S(1)}, bf16[512,512]{1,0:T(8,128)(2,1)S(1)}, u32[]{:S(2)}, u32[]{:S(2)}) collective-permute-start(bf16[512,512]{1,0:T(8,128)(2,1)S(1)} %all_gather.12.x0_ref), channel_id=1, source_target_pairs={{0,3},{1,0},{2,1},{3,2},{4,7},{5,4},{6,5},{7,6},{8,11},{9,8},{10,9... | collective-permute-start | bytes 1572872 | tf_op jit(solution)/shard_map/ppermute | solution.py:215

commit v7 on v5

--- a/solution.py
+++ b/solution.py
@@ -203,10 +203,11 @@
     hid, send = gelu_stage(pre, b_in, zh_n, x_n)
     got = lax.all_to_all(send, "x", 0, 0)
     rows = lax.all_gather(hid, ("y", "core"), axis=0, tiled=True)
-    outs = jnp.concatenate(
-        [dot_nn(rows[:, :f_loc], w_out).astype(bf16), dot_nt(rows[:, f_loc:], w_in).astype(bf16)],
-        axis=1,
-    )
+    first = dot_nn(rows[:, :f_loc], w_out).astype(bf16)
+    second = dot_nt(rows[:, f_loc:], w_in).astype(bf16)
+    outs = lax.optimization_barrier(jnp.zeros((rows.shape[0], 2 * d_loc), bf16))
+    outs = lax.dynamic_update_slice(outs, second, (0, d_loc))
+    outs = lax.dynamic_update_slice(outs, first, (0, 0))
     outs = lax.all_to_all(outs.reshape(2 * y_n, tile, 2 * d_loc), ("zq", "zp"), 0, 0)
     block_out, tokens_grad = final_stage(outs)
 

time: 129 us -> 130 us (level)
  the two profiles are of different devices: /device:TPU:7 before, /device:TPU:3 now
where the time goes in v7:
time: 130 us; the launch traced here: 129 us
  blocking collectives  61.7 us (47%)
  starting transfers between devices  32.9 us (25%)
  waiting for transfers between devices  20.8 us (16%)
  matrix products  4.71 us (4%)
  Pallas kernels  3.66 us (3%)
  local copies, waits for them, and re-layouts  2.24 us (2%)
  other arithmetic  2.07 us (2%)
    all_gather x1, blocking collectives, step(): zall = lax.all_gather(both, ('zh', 'zq', 'zp'), axis=0, tiled=True)  31 us
    all_gather x1, blocking collectives, step(): rows = lax.all_gather(hid, ('y', 'core'), axis=0, tiled=True)  15.6 us
    all_gather x1, blocking collectives, step(): wall = lax.all_gather(wsend, ('y', 'core'), axis=0, tiled=False)  15.1 us
    all_to_all x1, waiting for transfers between devices, step(): pre = lax.all_to_all(pre.reshape(y_n, zh_n * tile, 2 * f_loc), 'y', 0, 0)  13.1 us
    ppermute x1, starting transfers between devices, step(): from_core = lax.ppermute(first_products(1 - my_core, bf16), 'core', swap)  10.1 us
    ppermute x3, starting transfers between devices, step(): lax.ppermute(zall, 'x', [(i, (i + k) % x_n) for i in range(x_n)])  9.57 us
    ppermute x3, waiting for transfers between devices, step(): lax.ppermute(zall, 'x', [(i, (i + k) % x_n) for i in range(x_n)])  6.8 us
    all_to_all x1, starting transfers between devices, step(): lax.all_to_all(outs.reshape(2 * y_n, tile, 2 * d_loc), ('zq', 'zp'), 0, 0)  4.65 us
  transfers between devices with their start and end apart: 7, of which 3 were waited for; matrix products, arithmetic and copies ran while one was open for 3% of the time, Pallas kernels for 2%

profile of v7, /device:TPU:3, one launch (start us, length us, event | category | flops | bytes accessed | tf_op | source)
XLA Modules:
  0.0 128.9 jit_solution(4061260919697495776)
XLA Ops:
  0.6 0.0 copy-start
  0.7 0.9 pad_maximum_fusion.2
  1.5 31.0 %all_gather.12.x0_ref = bf16[512,512]{1,0:T(8,128)(2,1)S(1)} all-gather(bf16[32,512]{1,0:T(8,128)(2,1)S(1)} %pad_maximum_fusion.2), channel_id=1, replica_groups=mesh['y'=4,'core'=2,'zq'=4,'zp'=2,'zh'=2,'x'=4] {'zh','zq','zp'}, dimensions={0}, use_global_device_ids=true | all-gather | bytes 557056 | tf_op jit(solution)/shard_map/all_gather | solution.py:187
  32.5 0.0 copy-start.2
  32.6 1.4 %copy-done.2 = bf16[1792,512]{1,0:T(8,128)(2,1)S(1)} copy-done((bf16[1792,512]{1,0:T(8,128)(2,1)S(1)}, bf16[1792,512]{1,0:T(8,128)(2,1)}, u32[]{:S(2)}) %copy-start.2) | copy-done | bytes 1835032
  34.0 0.7 convolution_convert_fusion
  34.7 0.0 copy-done
  34.7 0.4 convolution_convert_fusion.1
  35.1 0.1 pad_maximum_fusion
  35.2 10.1 %collective-permute-start = (bf16[128,3584]{1,0:T(8,128)(2,1)S(1)}, bf16[128,3584]{1,0:T(8,128)(2,1)S(1)}, u32[]{:S(2)}, u32[]{:S(2)}) collective-permute-start(bf16[128,3584]{1,0:T(8,128)(2,1)S(1)} %pad_maximum_fusion), channel_id=1, source_target_pairs={{0,64},{64,0},{1,65},{65,1},{2,66},{66,2},{3,67},{67,3},{4,68},{68... | collective-permute-start | bytes 2752520 | tf_op jit(solution)/shard_map/ppermute | solution.py:200
  45.4 0.4 fusion.7
  45.8 0.7 fusion.8
  46.5 0.9 collective-permute-done
  47.4 1.1 fusion
  48.5 0.0 copy-start.1
  48.5 4.3 %all-to-all-start = ((bf16[4,32,3584]{2,1,0:T(8,128)(2,1)}), bf16[4,32,3584]{2,1,0:T(8,128)(2,1)S(1)}, u32[]{:S(2)}, u32[]{:S(2)}) async-start(bf16[4,32,3584]{2,1,0:T(8,128)(2,1)} %bitcast.33), calls=%async_computation | async-start | bytes 1835008 | tf_op jit(solution)/shard_map/all_to_all | solution.py:202
  52.8 13.1 %all-to-all-done.recv_ref = bf16[4,32,3584]{2,1,0:T(8,128)(2,1)S(1)} async-done(((bf16[4,32,3584]{2,1,0:T(8,128)(2,1)}), bf16[4,32,3584]{2,1,0:T(8,128)(2,1)S(1)}, u32[]{:S(2)}, u32[]{:S(2)}) %all-to-all-start) | async-done | bytes 917536 | tf_op jit(solution)/shard_map/all_to_all | solution.py:202
  66.0 0.0 copy-done.1
  66.0 1.1 gelu_stage.1
  67.0 4.3 %all-to-all-start.2 = ((bf16[4,40,448]{2,1,0:T(8,128)(2,1)}), bf16[4,40,448]{2,1,0:T(8,128)(2,1)S(1)}, u32[]{:S(2)}, u32[]{:S(2)}) async-start(bf16[4,40,448]{2,1,0:T(8,128)(2,1)} %get-tuple-element.15), calls=%async_computation.2 | async-start | bytes 327680 | tf_op jit(solution)/shard_map/all_to_all | solution.py:204
  71.3 0.0 copy-start.3
  71.3 15.6 %all_gather.13 = bf16[128,3584]{1,0:T(8,128)(2,1)S(1)} all-gather(bf16[16,3584]{1,0:T(8,128)(2,1)S(1)} %get-tuple-element.12), channel_id=1, replica_groups=mesh['y'=4,'core'=2,'zq'=4,'zp'=2,'zh'=2,'x'=4] {'y','core'}, dimensions={0}, use_global_device_ids=true | all-gather | bytes 1032192 | tf_op jit(solution)/shard_map/all_gather | solution.py:205
  86.9 0.7 broadcast_in_dim.3
  87.7 1.4 %fusion.2 = bf16[128,1024]{1,0:T(8,128)(2,1)} fusion(bf16[128,1024]{1,0:T(8,128)(2,1)} %broadcast_in_dim.3, bf16[512,1792]{1,0:T(8,128)(2,1)S(1)} %copy-done, bf16[128,3584]{1,0:T(8,128)(2,1)S(1)} %all_gather.13), kind=kOutput, calls=%fused_computation.7 | convolution fusion | flops 234946560 | bytes 2424832 | tf_op jit(solution)/shard_map/dot_general | solution.py:30
  89.1 0.0 copy-done.3
  89.1 1.1 fusion.1
  90.1 0.0 all-to-all-done.2
  90.1 4.6 %all-to-all-start.1 = ((bf16[8,16,1024]{2,1,0:T(8,128)(2,1)}), bf16[8,16,1024]{2,1,0:T(8,128)(2,1)S(1)}, u32[]{:S(2)}, u32[]{:S(2)}) async-start(bf16[8,16,1024]{2,1,0:T(8,128)(2,1)} %bitcast.13), calls=%async_computation.1 | async-start | bytes 524288 | tf_op jit(solution)/shard_map/all_to_all | solution.py:211
  94.8 3.1 %collective-permute-start.1 = (bf16[512,512]{1,0:T(8,128)(2,1)S(1)}, bf16[512,512]{1,0:T(8,128)(2,1)S(1)}, u32[]{:S(2)}, u32[]{:S(2)}) collective-permute-start(bf16[512,512]{1,0:T(8,128)(2,1)S(1)} %all_gather.12.x0_ref), channel_id=1, source_target_pairs={{0,1},{1,2},{2,3},{3,0},{4,5},{5,6},{6,7},{7,4},{8,9},{9,10},{10,1... | collective-permute-start | bytes 1572872 | tf_op jit(solution)/shard_map/ppermute | solution.py:190
  97.9 2.5 %collective-permute-start.2 = (bf16[512,512]{1,0:T(8,128)(2,1)S(1)}, bf16[512,512]{1,0:T(8,128)(2,1)S(1)}, u32[]{:S(2)}, u32[]{:S(2)}) collective-permute-start(bf16[512,512]{1,0:T(8,128)(2,1)S(1)} %all_gather.12.x0_ref), channel_id=1, source_target_pairs={{0,2},{1,3},{2,0},{3,1},{4,6},{5,7},{6,4},{7,5},{8,10},{9,11},{10,... | collective-permute-start | bytes 1572872 | tf_op jit(solution)/shard_map/ppermute | solution.py:190
  100.4 4.0 %collective-permute-start.3 = (bf16[512,512]{1,0:T(8,128)(2,1)S(1)}, bf16[512,512]{1,0:T(8,128)(2,1)S(1)}, u32[]{:S(2)}, u32[]{:S(2)}) collective-permute-start(bf16[512,512]{1,0:T(8,128)(2,1)S(1)} %all_gather.12.x0_ref), channel_id=1, source_target_pairs={{0,3},{1,0},{2,1},{3,2},{4,7},{5,4},{6,5},{7,6},{8,11},{9,8},{10,9... | collective-permute-start | bytes 1572872 | tf_op jit(solution)/shard_map/ppermute | solution.py:190
  104.5 15.1 %all-gather = bf16[1088,448]{1,0:T(8,128)(2,1)S(1)} all-gather(bf16[136,448]{1,0:T(8,128)(2,1)S(1)} %pad_maximum_fusion.1), channel_id=2, replica_groups=mesh['y'=4,'core'=2,'zq'=4,'zp'=2,'zh'=2,'x'=4] {'y','core'}, dimensions={0}, use_global_device_ids=true | all-gather | bytes 1096704 | tf_op jit(solution)/shard_map/all_gather | solution.py:218
  119.5 0.0 collective-permute-done.1.x1_ref
  119.5 0.0 collective-permute-done.2.x2_ref
  119.5 6.8 %collective-permute-done.3.x3_ref = bf16[512,512]{1,0:T(8,128)(2,1)S(1)} collective-permute-done((bf16[512,512]{1,0:T(8,128)(2,1)S(1)}, bf16[512,512]{1,0:T(8,128)(2,1)S(1)}, u32[]{:S(2)}, u32[]{:S(2)}) %collective-permute-start.3) | collective-permute-done | bytes 524320 | tf_op jit(solution)/shard_map/ppermute | solution.py:190
  126.3 1.9 %weight_stage.1 = (bf16[224,512]{1,0:T(8,128)(2,1)}, bf16[224,512]{1,0:T(8,128)(2,1)}, f32[14,128]{1,0:T(8,128)}) custom-call(bf16[512,512]{1,0:T(8,128)(2,1)S(1)} %all_gather.12.x0_ref, bf16[512,512]{1,0:T(8,128)(2,1)S(1)} %collective-permute-done.1.x1_ref, bf16[512,512]{1,0:T(8,128)(2,1)S(1)} %collective-permute-done.2.x2_ref, ...), custom_call_target="tpu_custom_call" | custom-call | tf_op jit(solution)/shard_map/weight_stage/pallas_call | solution.py:156
  128.3 0.0 all-to-all-done.1.parts_ref
  128.3 0.6 final_stage.1
  (8 shorter events, 0.2 us)
Async XLA Ops:
  0.6 34.1 %copy-start = (bf16[512,1792]{1,0:T(8,128)(2,1)S(1)}, bf16[512,1792]{1,0:T(8,128)(2,1)}, u32[]{:S(2)}) copy-start(bf16[512,1792]{1,0:T(8,128)(2,1)} %param.7) | copy-start | bytes 5505028
  32.5 1.5 %copy-start.2 = (bf16[1792,512]{1,0:T(8,128)(2,1)S(1)}, bf16[1792,512]{1,0:T(8,128)(2,1)}, u32[]{:S(2)}) copy-start(bf16[1792,512]{1,0:T(8,128)(2,1)} %param.9) | copy-start | bytes 5505028
  35.2 12.2 %collective-permute-start = (bf16[128,3584]{1,0:T(8,128)(2,1)S(1)}, bf16[128,3584]{1,0:T(8,128)(2,1)S(1)}, u32[]{:S(2)}, u32[]{:S(2)}) collective-permute-start(bf16[128,3584]{1,0:T(8,128)(2,1)S(1)} %pad_maximum_fusion), channel_id=1, source_target_pairs={{0,64},{64,0},{1,65},{65,1},{2,66},{66,2},{3,67},{67,3},{4,68},{68... | collective-permute-start | bytes 2752520 | tf_op jit(solution)/shard_map/ppermute | solution.py:200
  48.5 17.5 %copy-start.1 = (f32[1792]{0:T(1024)S(1)}, f32[1792]{0:T(1024)}, u32[]{:S(2)}) copy-start(f32[1792]{0:T(1024)} %param.8) | copy-start | bytes 21508
  48.5 17.4 %all-to-all-start = ((bf16[4,32,3584]{2,1,0:T(8,128)(2,1)}), bf16[4,32,3584]{2,1,0:T(8,128)(2,1)S(1)}, u32[]{:S(2)}, u32[]{:S(2)}) async-start(bf16[4,32,3584]{2,1,0:T(8,128)(2,1)} %bitcast.33), calls=%async_computation | async-start | bytes 1835008 | tf_op jit(solution)/shard_map/all_to_all | solution.py:202
  67.0 23.1 %all-to-all-start.2 = ((bf16[4,40,448]{2,1,0:T(8,128)(2,1)}), bf16[4,40,448]{2,1,0:T(8,128)(2,1)S(1)}, u32[]{:S(2)}, u32[]{:S(2)}) async-start(bf16[4,40,448]{2,1,0:T(8,128)(2,1)} %get-tuple-element.15), calls=%async_computation.2 | async-start | bytes 327680 | tf_op jit(solution)/shard_map/all_to_all | solution.py:204
  71.3 17.8 %copy-start.3 = (bf16[1792,512]{1,0:T(8,128)(2,1)S(1)}, bf16[1792,512]{1,0:T(8,128)(2,1)}, u32[]{:S(2)}) copy-start(bf16[1792,512]{1,0:T(8,128)(2,1)} %param.9) | copy-start | bytes 5505028
  90.1 38.2 %all-to-all-start.1 = ((bf16[8,16,1024]{2,1,0:T(8,128)(2,1)}), bf16[8,16,1024]{2,1,0:T(8,128)(2,1)S(1)}, u32[]{:S(2)}, u32[]{:S(2)}) async-start(bf16[8,16,1024]{2,1,0:T(8,128)(2,1)} %bitcast.13), calls=%async_computation.1 | async-start | bytes 524288 | tf_op jit(solution)/shard_map/all_to_all | solution.py:211
  94.8 24.8 %collective-permute-start.1 = (bf16[512,512]{1,0:T(8,128)(2,1)S(1)}, bf16[512,512]{1,0:T(8,128)(2,1)S(1)}, u32[]{:S(2)}, u32[]{:S(2)}) collective-permute-start(bf16[512,512]{1,0:T(8,128)(2,1)S(1)} %all_gather.12.x0_ref), channel_id=1, source_target_pairs={{0,1},{1,2},{2,3},{3,0},{4,5},{5,6},{6,7},{7,4},{8,9},{9,10},{10,1... | collective-permute-start | bytes 1572872 | tf_op jit(solution)/shard_map/ppermute | solution.py:190
  97.9 21.7 %collective-permute-start.2 = (bf16[512,512]{1,0:T(8,128)(2,1)S(1)}, bf16[512,512]{1,0:T(8,128)(2,1)S(1)}, u32[]{:S(2)}, u32[]{:S(2)}) collective-permute-start(bf16[512,512]{1,0:T(8,128)(2,1)S(1)} %all_gather.12.x0_ref), channel_id=1, source_target_pairs={{0,2},{1,3},{2,0},{3,1},{4,6},{5,7},{6,4},{7,5},{8,10},{9,11},{10,... | collective-permute-start | bytes 1572872 | tf_op jit(solution)/shard_map/ppermute | solution.py:190
  100.4 25.9 %collective-permute-start.3 = (bf16[512,512]{1,0:T(8,128)(2,1)S(1)}, bf16[512,512]{1,0:T(8,128)(2,1)S(1)}, u32[]{:S(2)}, u32[]{:S(2)}) collective-permute-start(bf16[512,512]{1,0:T(8,128)(2,1)S(1)} %all_gather.12.x0_ref), channel_id=1, source_target_pairs={{0,3},{1,0},{2,1},{3,2},{4,7},{5,4},{6,5},{7,6},{8,11},{9,8},{10,9... | collective-permute-start | bytes 1572872 | tf_op jit(solution)/shard_map/ppermute | solution.py:190
